TPU v7x, 32 devices: a whole 2x2x4 slice. The times are simulated.
32 devices in a mesh: mem: 4 (over y, core), gy: 4 (over z), gx: 2 (over x).
Axes of the slice: x: 2, y: 2, z: 4, core: 2. Of those that a mesh axis runs over, the one named last changes fastest.
Arguments:
- fields: float32 [20, 2, 256, 256], P('mem', None, 'gy', 'gx'), parts along dimension 0, may hold values from -6.5 to 6.5
- wind_x: float32 [8], P('mem'), parts along dimension 0, may hold values from -0.71 to 0.71
- wind_y: float32 [8], P('mem'), parts along dimension 0, may hold values from -0.71 to 0.71
- coupling: float32 [2, 5, 5], replicated, may hold values from -0.15 to 0.035
- north: bfloat16 [20, 2, 8, 256], P('mem'), parts along dimension 0, may hold values from -6 to 6
- south: bfloat16 [20, 2, 8, 256], P('mem'), parts along dimension 0, may hold values from -6 to 6
- west: bfloat16 [20, 2, 256, 8], P('mem'), parts along dimension 0, may hold values from -6 to 6
- east: bfloat16 [20, 2, 256, 8], P('mem'), parts along dimension 0, may hold values from -6 to 6
- strip_scale: float32 [16, 5, 2], P('mem'), parts along dimension 0, may hold values from 0.5 to 2
- widths: int32 [4], replicated, may hold values from 2 to 8, as said below
Outputs:
- advanced: float32 [20, 2, 256, 256], P('mem', None, 'gy', 'gx'), parts along dimension 0
There are 4 independent parts, one for each index of `mem`. A program takes and returns all parts, laid end to end along the dimension named above; an argument that names none is the same for every part. Nothing has to cross between parts.
Inputs may be any that keep to these rules, and one draw needn't show every extreme that they name: One of the four widths equals 8 in every draw.
All inputs are finite; a program needn't handle non-finite values.
Results may differ from a plain program's by a relative error of at most 0.0003.
Values sent between devices are 32-bit elements; how exact they have to be, the bound alone decides.
No kernel may reach another device: no remote copies, remote signals or barrier semaphores. Data moves between devices by JAX's collectives and lax.ppermute only.
A program may use at most 64 MiB of HBM per device.

v0:
```python
import functools

import jax
import jax.numpy as jnp
import numpy as np
from jax import lax
from jax.experimental import pallas as pl
from jax.experimental.pallas import tpu as pltpu
from jax.sharding import PartitionSpec as P

RELAX = 0.25
REACH = 3
HALO = 3 * REACH
PAD = 16
LANES = 128
FIRST = PAD - 8
THIRD, HALF = 1.0 / 3.0, 0.5

UPWIND = (-2.0, 15.0, -60.0, 20.0, 30.0, -3.0, 0.0)
CENTRAL = (-1.0, 9.0, -45.0, 0.0, 45.0, -9.0, 1.0)
DAMPING = (1.0, -6.0, 15.0, -20.0, 15.0, -6.0, 1.0)


def own_bands(cols):
    bands = np.zeros((2, LANES, LANES), np.float32)
    for col in range(cols):
        for offset in range(-REACH, REACH + 1):
            if 0 <= col + offset < cols:
                bands[0, col + offset, col] = UPWIND[offset + REACH]
                bands[1, col + offset, col] = -UPWIND[REACH - offset]
    return bands


def iota(shape, dim):
    return lax.broadcasted_iota(jnp.int32, shape, dim)


def edge_weight(distance, width):
    dist = distance.astype(jnp.float32)
    inside = (dist >= 0.0) & (dist < width)
    return jnp.where(inside, jnp.square((width - dist) / width), 0.0)


def slots(count_f, count_l):
    return [(f, l, HALO * (f * count_l + l)) for f in range(count_f) for l in range(count_l)]


def pack_y_kernel(fields, first_round, second_round):
    count_f, count_l, rows, _ = fields.shape
    even = lax.rem(lax.axis_index("gy"), 2) == 0
    for f, l, slot in slots(count_f, count_l):
        top = fields[f, l, 0:HALO, :]
        bottom = fields[f, l, rows - HALO : rows, :]
        first_round[slot : slot + HALO, :] = jnp.where(even, bottom, top)
        second_round[slot : slot + HALO, :] = jnp.where(even, top, bottom)


def halo_rows(gy_count, first_round, second_round, slot):
    gy = lax.axis_index("gy")
    even = lax.rem(gy, 2) == 0
    first = first_round[slot : slot + HALO, :]
    second = second_round[slot : slot + HALO, :]
    north = jnp.where(gy == 0, 0.0, jnp.where(even, second, first))
    south = jnp.where(gy == gy_count - 1, 0.0, jnp.where(even, first, second))
    return north, south


def sent_starts(gx_count, cols):
    if gx_count == 2:
        return [jnp.where(lax.axis_index("gx") == 0, cols - HALO, 0)]
    return [cols - HALO, 0]


def side_ids(gx_count):
    if gx_count == 2:
        return [jnp.where(lax.axis_index("gx") == 0, 0, 1)]
    return [1, 0]


def edge_starts(gx_count, cols):
    near = [jnp.where(side == 0, cols - HALO, 0) for side in side_ids(gx_count)]
    far = [jnp.where(side == 0, cols - HALO - REACH, HALO) for side in side_ids(gx_count)]
    return near, far


def level_weights(coupling, wind_x, wind_y, l, count_f):
    speed, size = wind_y[l] / 60.0, jnp.abs(wind_y[l]) / 60.0
    taps = [size * DAMPING[k] - speed * CENTRAL[k] for k in range(2 * REACH + 1)]
    mix = [
        [coupling[f, l, g] + (taps[REACH] if f == g else 0.0) for g in range(count_f)]
        for f in range(count_f)
    ]
    return [tap for k, tap in enumerate(taps) if k != REACH], mix, -wind_x[l] / 60.0


def side_bands(side, lane_speed, matrix):
    shape = (LANES, LANES)
    row, col = iota(shape, 0), iota(shape, 1)
    row_plane, col_plane = (row * 57) >> 9, (col * 57) >> 9
    apart = (row - HALO * row_plane) - (col - HALO * col_plane)
    apart = jnp.where(row_plane == col_plane, apart, 4 * HALO)
    sign = jnp.where(lane_speed > 0.0, -1, 1)
    sign_float = sign.astype(jnp.float32)

    def block(base):
        offset = (apart + base) * sign
        value = jnp.zeros(shape, jnp.float32)
        for k, entry in enumerate(UPWIND[:-1]):
            value = jnp.where(offset == k - REACH, entry, value)
        return (value * sign_float).astype(jnp.bfloat16)

    here, step = block(0), jnp.where(side == 0, HALO, -HALO)
    matrix[0:LANES, 0:LANES] = here
    matrix[LANES : 2 * LANES, LANES:] = here
    matrix[LANES : 2 * LANES, 0:LANES] = block(-step)
    matrix[0:LANES, LANES:] = block(step)
    matrix[2 * LANES :, 0:LANES] = jnp.zeros(shape, jnp.bfloat16)
    matrix[2 * LANES :, LANES:] = block(jnp.where(side == 0, -REACH, HALO))


def prepare_kernel(
    grid_sizes,
    fields,
    north,
    south,
    west,
    east,
    own_band,
    scale,
    widths,
    wind_x,
    wind_y,
    coupling,
    drive,
    relax,
    row_relax,
    inside,
    weights,
    lane_weights,
    own_matrix,
    *rest,
):
    gy_count, gx_count = grid_sizes
    sides = (len(rest) - 1) // 3
    payloads, side_drive, side_matrix = rest[:sides], rest[sides : 2 * sides], rest[2 * sides : -1]
    wide = rest[-1]
    count_f, count_l, rows, cols = fields.shape
    wide_rows = relax.shape[0]
    strip = north.shape[2]
    total_rows, total_cols = rows * gy_count, cols * gx_count
    gy, gx = lax.axis_index("gy"), lax.axis_index("gx")
    row_start, col_start = gy * rows, gx * cols
    width = [widths[s].astype(jnp.float32) for s in range(4)]
    lane = iota((8, LANES), 1)

    lane_rows = iota((rows, LANES), 1)
    starts = sent_starts(gx_count, cols)
    packed = [jnp.zeros((rows, LANES), jnp.float32) for _ in starts]
    if cols < LANES:
        wide[...] = jnp.zeros_like(wide)
    for f, l, slot in slots(count_f, count_l):
        if cols < LANES:
            wide[:, 0:cols] = fields[f, l]
            own = wide[...]
        else:
            own = fields[f, l]
        for n, start in enumerate(starts):
            moved = pltpu.roll(own, lax.rem(slot + LANES - start, LANES), 1)
            here = (lane_rows >= slot) & (lane_rows < slot + HALO)
            packed[n] = jnp.where(here, moved, packed[n])
    for payload, value in zip(payloads, packed):
        payload[...] = value

    def full(value):
        return jnp.full((8, LANES), value, jnp.float32)

    lane_taps = [full(0.0) for _ in range(2 * REACH)]
    lane_mix = [full(0.0) for _ in range(2 * count_f - 1)]
    lane_speed = full(0.0)
    for l in range(count_l):
        taps, mix, speed = level_weights(coupling, wind_x, wind_y, l, count_f)
        flat = taps + [entry for line in mix for entry in line] + [speed]
        for n, entry in enumerate(flat):
            weights[l, n] = full(entry)
        own_matrix[l] = own_band[jnp.where(wind_x[l] < 0.0, 1, 0)]
        for f in range(count_f):
            slot = HALO * (f * count_l + l)
            here = (lane >= slot) & (lane < slot + HALO)
            lane_taps = [jnp.where(here, tap, old) for tap, old in zip(taps, lane_taps)]
            lane_speed = jnp.where(here, speed, lane_speed)
            for g in range(count_f):
                at = g - f + count_f - 1
                lane_mix[at] = jnp.where(here, mix[f][g], lane_mix[at])
    for n, entry in enumerate(lane_taps + lane_mix + [lane_speed]):
        lane_weights[n] = entry
    for side, matrix in zip(side_ids(gx_count), side_matrix):
        side_bands(side, lane_speed[0:1, :], matrix)

    row_global = iota((wide_rows, LANES), 0) + (row_start - 8)
    row_weight = RELAX * (
        edge_weight(row_global, width[0]) + edge_weight(total_rows - 1 - row_global, width[1])
    )
    col_weight = RELAX * (
        edge_weight(lane + col_start, width[2])
        + edge_weight(total_cols - 1 - (lane + col_start), width[3])
    )
    row_relax[...] = row_weight
    relax[...] = row_weight + col_weight[0:1, :]
    inside[...] = jnp.where((row_global >= 0) & (row_global < total_rows), 1.0, 0.0)

    pos = iota((strip, LANES), 1)
    depth = iota((strip, LANES), 0)
    pick = jnp.concatenate([pos == depth, pos == depth + (cols - strip)], axis=0)
    pick = pick.astype(jnp.float32).astype(jnp.bfloat16)
    west_weight = RELAX * edge_weight(lane + col_start, width[2])
    east_weight = RELAX * edge_weight(total_cols - 1 - (lane + col_start), width[3])
    west_weight = jnp.where(lane < strip, west_weight, 0.0)
    east_weight = jnp.where((lane >= cols - strip) & (lane < cols), east_weight, 0.0)
    shift = lax.rem(8 + total_rows - row_start, total_rows)
    for f in range(count_f):
        for l in range(count_l):
            both = jnp.concatenate([west[f, l], east[f, l]], axis=0).astype(jnp.float32)
            both = pltpu.roll(both, shift, 1)[:, 0:LANES].astype(jnp.bfloat16)
            raw = lax.dot_general(
                both, pick, (((0,), (0,)), ((), ())), preferred_element_type=jnp.float32
            )
            factor = west_weight * scale[2, l, f] + east_weight * scale[3, l, f]
            drive[f, l] = raw[0:wide_rows] * factor[0:1, :]
    for ref in side_drive:
        ref[...] = jnp.zeros_like(ref)

    own_shift = lax.rem(total_cols - col_start, total_cols)
    for source, side, at, here in (
        (north, 0, 8, gy == 0),
        (south, 1, 8 + rows - strip, gy == gy_count - 1),
    ):

        @pl.when(here)
        def _(source=source, side=side, at=at):
            distance = depth if side == 0 else strip - 1 - depth
            weight = RELAX * edge_weight(distance, width[side])
            packed = [[jnp.zeros((strip, LANES), jnp.float32)] * 2 for _ in side_drive]
            for f, l, slot in slots(count_f, count_l):
                values = source[f, l].astype(jnp.float32)
                factor = weight * scale[side, l, f]
                own = pltpu.roll(values, own_shift, 1)[:, 0:LANES]
                drive[f, l, at : at + strip, :] = drive[f, l, at : at + strip, :] + factor * own
                held = (pos >= slot) & (pos < slot + HALO)
                for n, which in enumerate(side_ids(gx_count)):
                    for part, begin in enumerate(
                        (jnp.where(which == 0, cols, -HALO), jnp.where(which == 0, cols - HALO, 0))
                    ):
                        shift = slot + 2 * total_cols - begin - col_start
                        moved = pltpu.roll(values, lax.rem(shift, total_cols), 1)[:, 0:LANES]
                        packed[n][part] = jnp.where(held, factor * moved, packed[n][part])
            for ref, value in zip(side_drive, packed):
                for part in range(2):
                    ref[part, at : at + strip, :] = value[part]


def pack_x_kernel(grid_sizes, first_round, second_round, *rest):
    gy_count, gx_count = grid_sizes
    sides = (len(rest) - 1) // 2
    payloads, outs, ext = rest[:sides], rest[sides:-1], rest[-1]
    cols = first_round.shape[1]
    rows = payloads[0].shape[0]
    lane = iota((2 * PAD, LANES), 1)
    starts = sent_starts(gx_count, cols)
    packed = [jnp.zeros((2 * PAD, LANES), jnp.float32) for _ in starts]
    ext[...] = jnp.zeros_like(ext)
    for index in range(ext.shape[0]):
        slot = index * HALO
        north, south = halo_rows(gy_count, first_round, second_round, slot)
        ext[index, PAD - HALO : PAD, 0:cols] = north
        ext[index, PAD : PAD + HALO, 0:cols] = south
        for n, start in enumerate(starts):
            moved = pltpu.roll(ext[index], lax.rem(slot + LANES - start, LANES), 1)
            packed[n] = jnp.where((lane >= slot) & (lane < slot + HALO), moved, packed[n])
    for out, payload, value in zip(outs, payloads, packed):
        out[0:PAD, :] = value[0:PAD]
        out[PAD : PAD + rows, :] = payload[...]
        out[PAD + rows : 2 * PAD + rows, :] = value[PAD : 2 * PAD]


def loaded(weights, l, fac, count_f):
    flat = [fac * weights[l, n] for n in range(weights.shape[1])]
    taps, flat, speed = flat[: 2 * REACH], flat[2 * REACH : -1], flat[-1]
    return taps, [flat[f * count_f : (f + 1) * count_f] for f in range(count_f)], speed


def y_terms(rows_at, at, taps, total):
    offsets = [k for k in range(-REACH, REACH + 1) if k != 0]
    for tap, offset in zip(taps, offsets):
        total = total + tap * rows_at(at + offset)
    return total


def cell_terms(src, l, f, at, centers, weight, taps, mix, total):
    for g, center in enumerate(centers):
        total = total + (mix[f][g] - weight if g == f else mix[f][g]) * center
    return y_terms(lambda row: src[f, l, pl.ds(row, 8), :], at, taps, total)


def split(value):
    high = value.astype(jnp.bfloat16)
    return high, (value - high.astype(jnp.float32)).astype(jnp.bfloat16)


def x_divergence(src, l, first, height, matrix, xdiv):
    count_f = src.shape[0]
    whole = src[:, l, first : first + height, :].reshape(count_f * height, LANES)
    both = jnp.concatenate(split(whole), axis=1)
    twice = jnp.concatenate([matrix[l], matrix[l]], axis=0)
    moved = jnp.dot(both, twice, preferred_element_type=jnp.float32)
    xdiv[:, 0:height, :] = moved.reshape(count_f, height, LANES)


def begin_kernel(
    grid_sizes,
    fields,
    first_round,
    second_round,
    drive,
    relax,
    weights,
    own_matrix,
    after,
    *rest,
):
    gy_count, gx_count = grid_sizes
    far, (state, own_one, own_two, xdiv) = rest[:-4], rest[-4:]
    count_f, count_l, rows, cols = fields.shape
    wide_rows = relax.shape[0]
    gy = lax.axis_index("gy")
    pad_rows = jnp.zeros((PAD, LANES), jnp.float32)
    for f, l, slot in slots(count_f, count_l):
        north, south = halo_rows(gy_count, first_round, second_round, slot)
        if cols < LANES:
            state[f, l] = jnp.zeros(state.shape[2:], jnp.float32)
        else:
            state[f, l, 0:PAD, :] = pad_rows
            state[f, l, PAD + rows : 2 * PAD + rows, :] = pad_rows
        state[f, l, PAD - HALO : PAD, 0:cols] = north
        state[f, l, PAD : PAD + rows, 0:cols] = fields[f, l]
        state[f, l, PAD + rows : PAD + rows + HALO, 0:cols] = south
    lane = iota((wide_rows, LANES), 1)
    starts = edge_starts(gx_count, cols)[1]

    def keep_far(src, section):
        for ref, start in zip(far, starts):
            packed = jnp.zeros((wide_rows, LANES), jnp.float32)
            here = (lane >= start) & (lane < start + REACH)
            for f, l, slot in slots(count_f, count_l):
                kept = jnp.where(here, src[f, l, FIRST : FIRST + wide_rows, :], 0.0)
                packed = packed + pltpu.roll(kept, lax.rem(slot + LANES - start, LANES), 1)
            ref[section] = packed

    keep_far(state, 0)
    for section, (src, dst, fac) in enumerate(
        ((state, own_one, THIRD), (own_one, own_two, HALF), (own_two, after, 1.0))
    ):
        first, height = (PAD, rows) if dst is after else (FIRST, wide_rows)
        for l in range(count_l):
            x_divergence(src, l, first, height, own_matrix, xdiv)
            taps, mix, speed = loaded(weights, l, fac, count_f)
            for n in range(height // 8):
                at, row = first + n * 8, n * 8
                to = at - FIRST
                centers = [src[g, l, at : at + 8, :] for g in range(count_f)]
                weight = fac * relax[to : to + 8, :]
                for f in range(count_f):
                    base = centers[f] if src is state else state[f, l, at : at + 8, :]
                    total = base + fac * drive[f, l, to : to + 8, :]
                    total = total + speed * xdiv[f, row : row + 8, :]
                    total = cell_terms(src, l, f, at, centers, weight, taps, mix, total)
                    if dst is after:
                        after[f, l, row : row + 8, :] = total[:, 0:cols]
                    else:
                        dst[f, l, at : at + 8, :] = total
        if dst is not after:
            for row, here in ((FIRST, gy == 0), (PAD + rows, gy == gy_count - 1)):

                @pl.when(here)
                def _(dst=dst, row=row):
                    dst[:, :, row : row + 8, :] = jnp.zeros(
                        (count_f, count_l, 8, LANES), jnp.float32
                    )

            keep_far(dst, section + 1)


def finish_kernel(grid_sizes, sides, *refs):
    gy_count, gx_count = grid_sizes
    halos, edges, fars, side_drive, side_matrix = (
        refs[n * sides : (n + 1) * sides] for n in range(5)
    )
    after, row_relax, inside, lane_weights, out, one, two, xdiv = refs[5 * sides :]
    count_f, count_l, rows, cols = out.shape
    wide_rows = row_relax.shape[0]
    gx = lax.axis_index("gx")
    starts = edge_starts(gx_count, cols)[0]
    exists = [None] if sides == 1 else [gx > 0, gx < gx_count - 1]
    taps = [lane_weights[k] for k in range(2 * REACH)]
    mix = [lane_weights[2 * REACH + d] for d in range(2 * count_f - 1)]
    speed = lane_weights[lane_weights.shape[0] - 1]

    def section(parts, s, fac, number, first, height, wanted, store):
        columns = [part[first : first + height, :] for part in parts]
        columns.append(fars[s][number, first - FIRST : first - FIRST + height, :])
        both = jnp.concatenate(split(jnp.concatenate(columns, axis=1)), axis=0)
        moved = jnp.dot(
            both, side_matrix[s][:, wanted[0] * LANES :], preferred_element_type=jnp.float32
        )
        moved = moved[0:height] + moved[height:]
        for n, which in enumerate(wanted):
            xdiv[which, 0:height, :] = moved[:, n * LANES : (n + 1) * LANES]
        for which in wanted:
            part, start = parts[which], (halos, edges)[which][s]
            for n in range(height // 8):
                at, row = first + n * 8, n * 8
                to = at - FIRST
                center = part[at : at + 8, :]
                rate = side_drive[s][which, to : to + 8, :] + speed * xdiv[which, row : row + 8, :]
                rate = rate - row_relax[to : to + 8, :] * center
                for d, entry in enumerate(mix):
                    step = (d - (count_f - 1)) * HALO * count_l
                    other = pltpu.roll(center, -step % LANES, 1) if step else center
                    rate = rate + entry * other
                rate = y_terms(lambda row: part[row : row + 8, :], at, taps, rate)
                store(which, at, to, start[at : at + 8, :] + fac * rate)

    lane = iota((rows, LANES), 1)
    for s in range(sides):
        def keep(ref):
            def store(which, at, to, value):
                kept = inside[to : to + 8, :]
                if exists[s] is not None and which == 0:
                    kept = jnp.where(exists[s], kept, 0.0)
                ref[which, at : at + 8, :] = value * kept

            return store

        section((halos[s], edges[s]), s, THIRD, 0, FIRST, wide_rows, (0, 1), keep(one))
        section((one.at[0], one.at[1]), s, HALF, 1, FIRST, wide_rows, (0, 1), keep(two))

        def last(which, at, to, value):
            one[0, at : at + 8, :] = value

        section((two.at[0], two.at[1]), s, 1.0, 2, PAD, rows, (1,), last)
        right = one[0, PAD : PAD + rows, :]
        near = (lane >= starts[s]) & (lane < starts[s] + HALO)
        if exists[s] is not None:
            near = near & exists[s]
        source = after if s == 0 else out
        for f, l, slot in slots(count_f, count_l):
            moved = pltpu.roll(right, lax.rem(starts[s] + LANES - slot, LANES), 1)
            out[f, l] = jnp.where(near[:, 0:cols], moved[:, 0:cols], source[f, l])


def pair_rounds(gy_count, gx_count):
    rounds = []
    for start in (0, 1):
        partner = {}
        for low in range(start, gy_count - 1, 2):
            partner[low], partner[low + 1] = low + 1, low
        pairs = []
        for y in range(gy_count):
            for x in range(gx_count):
                if y in partner:
                    pairs.append((y * gx_count + x, partner[y] * gx_count + x))
                elif gx_count % 2 == 0:
                    pairs.append((y * gx_count + x, y * gx_count + (x ^ 1)))
        rounds.append(pairs)
    return rounds


def local(
    gy_count, gx_count, fields, wind_x, wind_y, coupling, north, south, west, east, strip_scale, widths
):
    count_f, count_l, rows, cols = fields.shape
    ext_rows = rows + 2 * PAD
    grid_sizes = (gy_count, gx_count)
    packed_rows = -(-HALO * count_f * count_l // 8) * 8
    vmem = pl.BlockSpec(memory_space=pltpu.VMEM)
    smem = pl.BlockSpec(memory_space=pltpu.SMEM)
    f32 = functools.partial(jax.ShapeDtypeStruct, dtype=jnp.float32)

    def call(body, name, out_shape, inputs, scratch=(), limit=4):
        several = isinstance(out_shape, tuple)
        return pl.pallas_call(
            body,
            out_shape=out_shape,
            in_specs=[space for _, space in inputs],
            out_specs=(vmem,) * len(out_shape) if several else vmem,
            scratch_shapes=list(scratch),
            compiler_params=pltpu.CompilerParams(vmem_limit_bytes=limit << 20),
            name=name,
        )(*[value for value, _ in inputs])

    def inputs(space, *values):
        return [(value, space) for value in values]

    strip_shape = f32((packed_rows, cols))
    sent_first, sent_second = call(
        pack_y_kernel, "pack_y", (strip_shape, strip_shape), inputs(vmem, fields)
    )
    first_pairs, second_pairs = pair_rounds(gy_count, gx_count)
    first_round = lax.ppermute(sent_first, ("gy", "gx"), first_pairs)
    second_round = lax.ppermute(sent_second, ("gy", "gx"), second_pairs)

    mixing = jnp.transpose(coupling, (1, 0, 2))
    scales = jnp.transpose(strip_scale, (0, 2, 1))
    sides = 1 if gx_count == 2 else 2
    wide_rows = rows + 16
    state_shape = (count_f, count_l, ext_rows, LANES)
    wide_shape = (count_f, count_l, wide_rows, LANES)
    plane = f32((wide_rows, LANES))
    matrix = functools.partial(jax.ShapeDtypeStruct, dtype=jnp.bfloat16)
    entries = 2 * REACH + count_f * count_f + 1
    lane_entries = 2 * REACH + 2 * count_f
    prepared = call(
        functools.partial(prepare_kernel, grid_sizes),
        "prepare",
        (f32(wide_shape), plane, plane, plane)
        + (f32((count_l, entries, 8, LANES)), f32((lane_entries, 8, LANES)))
        + (matrix((count_l, LANES, LANES)),)
        + (f32((rows, LANES)),) * sides
        + (f32((2, wide_rows, LANES)),) * sides
        + (matrix((3 * LANES, 2 * LANES)),) * sides,
        inputs(vmem, fields, north, south, jnp.swapaxes(west, 2, 3), jnp.swapaxes(east, 2, 3))
        + inputs(vmem, jnp.asarray(own_bands(cols), jnp.bfloat16))
        + inputs(smem, scales, widths, wind_x, wind_y, mixing),
        scratch=[pltpu.VMEM((rows, LANES), jnp.float32)],
    )
    drive, relax, row_relax, inside, weights, lane_weights, own_matrix = prepared[:7]
    payloads, side_drive, side_matrix = (
        prepared[7 + n * sides : 7 + (n + 1) * sides] for n in range(3)
    )

    sent = call(
        functools.partial(pack_x_kernel, grid_sizes),
        "pack_x",
        (f32((ext_rows, LANES)),) * sides,
        inputs(vmem, first_round, second_round, *payloads),
        scratch=[pltpu.VMEM((count_f * count_l, 2 * PAD, LANES), jnp.float32)],
    )
    forward = [(i, i + 1) for i in range(gx_count - 1)]
    backward = [(b, a) for a, b in forward]
    if sides == 1:
        halos = [lax.ppermute(sent[0], "gx", forward + backward)]
    else:
        halos = [lax.ppermute(sent[0], "gx", forward), lax.ppermute(sent[1], "gx", backward)]

    state = pltpu.VMEM(state_shape, jnp.float32)
    after, *far = call(
        functools.partial(begin_kernel, grid_sizes),
        "begin",
        (f32(fields.shape),) + (f32((3, wide_rows, LANES)),) * sides,
        inputs(vmem, fields, first_round, second_round, drive, relax, weights, own_matrix),
        scratch=[state] * 3 + [pltpu.VMEM((count_f, wide_rows, LANES), jnp.float32)],
        limit=8,
    )
    pair = pltpu.VMEM((2, ext_rows, LANES), jnp.float32)
    return call(
        functools.partial(finish_kernel, grid_sizes, sides),
        "finish",
        f32(fields.shape),
        inputs(vmem, *halos, *sent[::-1], *far, *side_drive, *side_matrix)
        + inputs(vmem, after, row_relax, inside, lane_weights),
        scratch=[pair, pair, pltpu.VMEM((2, wide_rows, LANES), jnp.float32)],
    )


def solution(mesh):
    return jax.shard_map(
        functools.partial(local, mesh.shape["gy"], mesh.shape["gx"]),
        mesh=mesh,
        in_specs=(
            P("mem", None, "gy", "gx"),
            P("mem"),
            P("mem"),
            P(),
            P("mem", None, None, None),
            P("mem", None, None, None),
            P("mem", None, None, None),
            P("mem", None, None, None),
            P("mem", None, None),
            P(),
        ),
        out_specs=P("mem", None, "gy", "gx"),
        check_vma=False,
    )
```

profile of v0, /device:TPU:0, one launch (start us, length us, event | category | flops | bytes accessed | tf_op | source)
XLA Modules:
  0.0 14.2 jit_solution(14461845058677174617)
XLA Ops:
  0.0 0.0 copy-start
  0.0 1.0 %copy-done = f32[5,2,64,128]{3,2,1,0:T(8,128)S(1)} copy-done((f32[5,2,64,128]{3,2,1,0:T(8,128)S(1)}, f32[5,2,64,128]{3,2,1,0:T(8,128)}, u32[]{:S(2)}) %copy-start) | copy-done | bytes 327704
  1.0 0.0 copy-start.2
  1.0 0.0 copy-start.3
  1.0 0.0 copy-start.4
  1.0 0.0 copy-start.6
  1.0 0.0 copy-start.9
  1.0 0.0 copy-start.10
  1.0 0.0 copy-start.11
  1.1 0.0 copy-start.7
  1.1 3.1 %collective-permute-start = (f32[96,128]{1,0:T(8,128)S(1)}, f32[96,128]{1,0:T(8,128)S(1)}, u32[]{:S(2)}, u32[]{:S(2)}) collective-permute-start(f32[96,128]{1,0:T(8,128)S(1)} %get-tuple-element.19), channel_id=1, source_target_pairs={{0,2},{1,3},{2,0},{3,1},{4,6},{5,7},{6,4},{7,5},{8,10},{9,11},{10,... | collective-permute-start | bytes 147464 | tf_op jit(solution)/shard_map/ppermute | solution.py:508
  4.2 1.5 %collective-permute-start.1 = (f32[96,128]{1,0:T(8,128)S(1)}, f32[96,128]{1,0:T(8,128)S(1)}, u32[]{:S(2)}, u32[]{:S(2)}) collective-permute-start(f32[96,128]{1,0:T(8,128)S(1)} %get-tuple-element.20), channel_id=1, source_target_pairs={{0,1},{1,0},{2,4},{3,5},{4,2},{5,3},{6,7},{7,6},{8,9},{9,8},{10,12... | collective-permute-start | bytes 147464 | tf_op jit(solution)/shard_map/ppermute | solution.py:509
  5.7 0.0 copy-done.2
  5.7 0.0 copy-done.3
  5.7 0.0 copy-done.4
  5.7 0.0 copy-done.5
  5.7 0.0 copy-done.6
  5.7 0.0 copy-done.9
  5.7 0.0 copy-done.10
  5.7 0.0 copy-done.11
  5.7 0.0 copy-done.7
  5.7 0.0 copy-done.8
  5.8 0.0 copy-start.1
  5.8 1.3 %prepare.1 = (f32[5,2,80,128]{3,2,1,0:T(8,128)S(1)}, f32[80,128]{1,0:T(8,128)S(1)}, f32[80,128]{1,0:T(8,128)S(1)}, f32[80,128]{1,0:T(8,128)S(1)}, f32[2,32,8,128...) custom-call(f32[5,2,64,128]{3,2,1,0:T(8,128)S(1)} %copy-done, ...), custom_call_target="tpu_custom_call" | custom-call | tf_op jit(solution)/shard_map/prepare/pallas_call | solution.py:490
  7.1 0.0 collective-permute-done.first_round
  7.1 1.1 %collective-permute-done.1.second_round = f32[96,128]{1,0:T(8,128)S(1)} collective-permute-done((f32[96,128]{1,0:T(8,128)S(1)}, f32[96,128]{1,0:T(8,128)S(1)}, u32[]{:S(2)}, u32[]{:S(2)}) %collective-permute-start.1) | collective-permute-done | bytes 49184 | tf_op jit(solution)/shard_map/ppermute | solution.py:509
  8.3 0.1 pack_x.1.refs_1_
  8.4 1.6 %collective-permute-start.2 = (f32[96,128]{1,0:T(8,128)S(1)}, f32[96,128]{1,0:T(8,128)S(1)}, u32[]{:S(2)}, u32[]{:S(2)}) collective-permute-start(f32[96,128]{1,0:T(8,128)S(1)} %pack_x.1.refs_1_), channel_id=1, source_target_pairs={{0,1},{1,0},{2,3},{3,2},{4,5},{5,4},{6,7},{7,6},{8,9},{9,8},{10,11... | collective-permute-start | bytes 147464 | tf_op jit(solution)/shard_map/ppermute | solution.py:550
  10.0 0.0 copy-done.1
  10.0 2.1 %begin.1 = (f32[5,2,64,128]{3,2,1,0:T(8,128)S(1)}, f32[3,80,128]{2,1,0:T(8,128)S(1)}) custom-call(f32[5,2,64,128]{3,2,1,0:T(8,128)S(1)} %copy-done.1, f32[96,128]{1,0:T(8,128)S(1)} %collective-permute-done.first_round, f32[96,128]{1,0:T(8,128)S(1)} %collective-permute-done.1.second_round, f32[5,2,80,128]{3,2,1,0:T(8,128)S(1)} %get-tuple-element.22.drive, ...), custom_call_target="tpu_custom_call" | custom-call | tf_op jit(solution)/shard_map/begin/pallas_call | solution.py:490
  12.1 0.5 %collective-permute-done.2.refs_0_ = f32[96,128]{1,0:T(8,128)S(1)} collective-permute-done((f32[96,128]{1,0:T(8,128)S(1)}, f32[96,128]{1,0:T(8,128)S(1)}, u32[]{:S(2)}, u32[]{:S(2)}) %collective-permute-start.2) | collective-permute-done | bytes 49184 | tf_op jit(solution)/shard_map/ppermute | solution.py:550
  12.6 1.6 %finish.1 = f32[5,2,64,128]{3,2,1,0:T(8,128)} custom-call(f32[96,128]{1,0:T(8,128)S(1)} %collective-permute-done.2.refs_0_, f32[96,128]{1,0:T(8,128)S(1)} %pack_x.1.refs_1_, f32[3,80,128]{2,1,0:T(8,128)S(1)} %get-tuple-element.26.refs_2_, f32[2,80,128]{2,1,0:T(8,128)S(1)} %get-tuple-element.27.refs_3_, bf16[384,256]{1,0:T(8,128)(2,1)S(1)} %get-tuple-element.28.refs_4_, ...), custom_call_target="tpu_custom_call" | custom-call | tf_op jit(solution)/shard_map/finish/pallas_call | solution.py:490
  (3 shorter events, 0.0 us)
Async XLA Ops:
  0.0 1.0 %copy-start = (f32[5,2,64,128]{3,2,1,0:T(8,128)S(1)}, f32[5,2,64,128]{3,2,1,0:T(8,128)}, u32[]{:S(2)}) copy-start(f32[5,2,64,128]{3,2,1,0:T(8,128)} %fields.5) | copy-start | bytes 983044
  1.0 4.7 %copy-start.2 = (bf16[2,128,128]{2,1,0:T(8,128)(2,1)S(1)}, bf16[2,128,128]{2,1,0:T(8,128)(2,1)}, u32[]{:S(2)}) copy-start(bf16[2,128,128]{2,1,0:T(8,128)(2,1)} %constant.2.clone.own_band) | copy-start | bytes 196612
  1.0 4.7 %copy-start.3 = (bf16[5,2,8,256]{3,2,1,0:T(8,128)(2,1)S(1)}, bf16[5,2,8,256]{3,2,1,0:T(8,128)(2,1)}, u32[]{:S(2)}) copy-start(bf16[5,2,8,256]{3,2,1,0:T(8,128)(2,1)} %north.1) | copy-start | bytes 122884
  1.0 4.7 %copy-start.4 = (bf16[5,2,8,256]{3,2,1,0:T(8,128)(2,1)S(1)}, bf16[5,2,8,256]{3,2,1,0:T(8,128)(2,1)}, u32[]{:S(2)}) copy-start(bf16[5,2,8,256]{3,2,1,0:T(8,128)(2,1)} %south.1) | copy-start | bytes 122884
  1.0 4.7 %copy-start.5 = (bf16[5,2,256,8]{2,3,1,0:T(8,128)(2,1)S(1)}, bf16[5,2,256,8]{2,3,1,0:T(8,128)(2,1)}, u32[]{:S(2)}) copy-start(bf16[5,2,256,8]{2,3,1,0:T(8,128)(2,1)} %param.17) | copy-start | bytes 122884
  1.0 4.7 %copy-start.6 = (bf16[5,2,256,8]{2,3,1,0:T(8,128)(2,1)S(1)}, bf16[5,2,256,8]{2,3,1,0:T(8,128)(2,1)}, u32[]{:S(2)}) copy-start(bf16[5,2,256,8]{2,3,1,0:T(8,128)(2,1)} %param.18) | copy-start | bytes 122884
  1.0 4.7 %copy-start.9 = (s32[4]{0:T(128)S(1)}, s32[4]{0:T(128)}, u32[]{:S(2)}) copy-start(s32[4]{0:T(128)} %widths.1) | copy-start | bytes 52
  1.0 4.7 %copy-start.10 = (f32[2]{0:T(128)S(1)}, f32[2]{0:T(128)}, u32[]{:S(2)}) copy-start(f32[2]{0:T(128)} %wind_x.1) | copy-start | bytes 28
  1.0 4.7 %copy-start.11 = (f32[2]{0:T(128)S(1)}, f32[2]{0:T(128)}, u32[]{:S(2)}) copy-start(f32[2]{0:T(128)} %wind_y.1) | copy-start | bytes 28
  1.1 4.7 %copy-start.7 = (f32[2,5,5]{2,0,1:T(2,128)S(1)}, f32[2,5,5]{2,0,1:T(2,128)}, u32[]{:S(2)}) copy-start(f32[2,5,5]{2,0,1:T(2,128)} %param.14) | copy-start | bytes 604
  1.1 6.1 %collective-permute-start = (f32[96,128]{1,0:T(8,128)S(1)}, f32[96,128]{1,0:T(8,128)S(1)}, u32[]{:S(2)}, u32[]{:S(2)}) collective-permute-start(f32[96,128]{1,0:T(8,128)S(1)} %get-tuple-element.19), channel_id=1, source_target_pairs={{0,2},{1,3},{2,0},{3,1},{4,6},{5,7},{6,4},{7,5},{8,10},{9,11},{10,... | collective-permute-start | bytes 147464 | tf_op jit(solution)/shard_map/ppermute | solution.py:508
  4.2 1.6 %copy-start.8 = (f32[4,5,2]{1,2,0:T(2,128)S(1)}, f32[4,5,2]{1,2,0:T(2,128)}, u32[]{:S(2)}) copy-start(f32[4,5,2]{1,2,0:T(2,128)} %param.19) | copy-start | bytes 484
  4.2 4.1 %collective-permute-start.1 = (f32[96,128]{1,0:T(8,128)S(1)}, f32[96,128]{1,0:T(8,128)S(1)}, u32[]{:S(2)}, u32[]{:S(2)}) collective-permute-start(f32[96,128]{1,0:T(8,128)S(1)} %get-tuple-element.20), channel_id=1, source_target_pairs={{0,1},{1,0},{2,4},{3,5},{4,2},{5,3},{6,7},{7,6},{8,9},{9,8},{10,12... | collective-permute-start | bytes 147464 | tf_op jit(solution)/shard_map/ppermute | solution.py:509
  5.8 4.2 %copy-start.1 = (f32[5,2,64,128]{3,2,1,0:T(8,128)S(1)}, f32[5,2,64,128]{3,2,1,0:T(8,128)}, u32[]{:S(2)}) copy-start(f32[5,2,64,128]{3,2,1,0:T(8,128)} %fields.5) | copy-start | bytes 983044
  8.4 4.2 %collective-permute-start.2 = (f32[96,128]{1,0:T(8,128)S(1)}, f32[96,128]{1,0:T(8,128)S(1)}, u32[]{:S(2)}, u32[]{:S(2)}) collective-permute-start(f32[96,128]{1,0:T(8,128)S(1)} %pack_x.1.refs_1_), channel_id=1, source_target_pairs={{0,1},{1,0},{2,3},{3,2},{4,5},{5,4},{6,7},{7,6},{8,9},{9,8},{10,11... | collective-permute-start | bytes 147464 | tf_op jit(solution)/shard_map/ppermute | solution.py:550
where the time goes:
time: 14.3 us; the launch traced here: 14.2 us
  starting transfers between devices  6.16 us (43%)
  Pallas kernels  5.21 us (36%)
  waiting for transfers between devices  1.65 us (12%)
  local copies, waits for them, and re-layouts  1.02 us (7%)
  between operations  0.15 us (1%)
    pallas_call x5, Pallas kernels, call(): pl.pallas_call(body, out_shape=out_shape, in_specs=[space for _, space in...  5.21 us
    ppermute x1, starting transfers between devices, local(): first_round = lax.ppermute(sent_first, ('gy', 'gx'), first_pairs)  3.12 us
    ppermute x1, starting transfers between devices, local(): halos = [lax.ppermute(sent[0], 'gx', forward + backward)]  1.56 us
    ppermute x1, starting transfers between devices, local(): second_round = lax.ppermute(sent_second, ('gy', 'gx'), second_pairs)  1.49 us
    ppermute x1, waiting for transfers between devices, local(): second_round = lax.ppermute(sent_second, ('gy', 'gx'), second_pairs)  1.15 us
    unnamed x24, local copies, waits for them, and re-layouts  1.02 us
    ppermute x1, waiting for transfers between devices, local(): halos = [lax.ppermute(sent[0], 'gx', forward + backward)]  0.49 us
  transfers between devices with their start and end apart: 3, of which 2 were waited for; matrix products, arithmetic and copies ran while one was open for 0% of the time, Pallas kernels for 24%

commit v1 on v0

--- a/solution.py
+++ b/solution.py
@@ -457,19 +457,25 @@
             out[f, l] = jnp.where(near[:, 0:cols], moved[:, 0:cols], source[f, l])
 
 
-def pair_rounds(gy_count, gx_count):
+def pair_rounds(part_count, gy_count, gx_count):
     rounds = []
     for start in (0, 1):
         partner = {}
         for low in range(start, gy_count - 1, 2):
             partner[low], partner[low + 1] = low + 1, low
         pairs = []
-        for y in range(gy_count):
-            for x in range(gx_count):
-                if y in partner:
-                    pairs.append((y * gx_count + x, partner[y] * gx_count + x))
-                elif gx_count % 2 == 0:
-                    pairs.append((y * gx_count + x, y * gx_count + (x ^ 1)))
+        for place in np.ndindex(part_count, gy_count, gx_count):
+            part, y, x = place
+            if y in partner:
+                to = part, partner[y], x
+            elif part_count % 2 == 0:
+                to = part ^ 1, y, x
+            elif gx_count % 2 == 0:
+                to = part, y, x ^ 1
+            else:
+                continue
+            shape = (part_count, gy_count, gx_count)
+            pairs.append(tuple(int(np.ravel_multi_index(at, shape)) for at in (place, to)))
         rounds.append(pairs)
     return rounds
 
@@ -504,9 +510,10 @@
     sent_first, sent_second = call(
         pack_y_kernel, "pack_y", (strip_shape, strip_shape), inputs(vmem, fields)
     )
-    first_pairs, second_pairs = pair_rounds(gy_count, gx_count)
-    first_round = lax.ppermute(sent_first, ("gy", "gx"), first_pairs)
-    second_round = lax.ppermute(sent_second, ("gy", "gx"), second_pairs)
+    axes = ("mem", "gy", "gx")
+    first_pairs, second_pairs = pair_rounds(lax.axis_size("mem"), gy_count, gx_count)
+    first_round = lax.ppermute(sent_first, axes, first_pairs)
+    second_round = lax.ppermute(sent_second, axes, second_pairs)
 
     mixing = jnp.transpose(coupling, (1, 0, 2))
     scales = jnp.transpose(strip_scale, (0, 2, 1))

time: 14.3 us -> 12.9 us (0.902)
  the two profiles are of different devices: /device:TPU:0 before, /device:TPU:18 now
where the time goes in v1:
time: 12.9 us; the launch traced here: 12.7 us
  Pallas kernels  5.08 us (39%)
  waiting for transfers between devices  3.63 us (28%)
  starting transfers between devices  2.24 us (17%)
  local copies, waits for them, and re-layouts  1.62 us (13%)
  between operations  0.14 us (1%)
    pallas_call x5, Pallas kernels, call(): pl.pallas_call(body, out_shape=out_shape, in_specs=[space for _, space in...  5.08 us
    ppermute x1, starting transfers between devices, local(): first_round = lax.ppermute(sent_first, axes, first_pairs)  1.64 us
    unnamed x24, local copies, waits for them, and re-layouts  1.62 us
    ppermute x1, waiting for transfers between devices, local(): second_round = lax.ppermute(sent_second, axes, second_pairs)  1.58 us
    ppermute x1, waiting for transfers between devices, local(): halos = [lax.ppermute(sent[0], 'gx', forward + backward)]  1.45 us
    ppermute x1, waiting for transfers between devices, local(): first_round = lax.ppermute(sent_first, axes, first_pairs)  0.6 us
    ppermute x1, starting transfers between devices, local(): halos = [lax.ppermute(sent[0], 'gx', forward + backward)]  0.6 us
  transfers between devices with their start and end apart: 3, of which 3 were waited for; matrix products, arithmetic and copies ran while one was open for 0% of the time, Pallas kernels for 26%

profile of v1, /device:TPU:18, one launch (start us, length us, event | category | flops | bytes accessed | tf_op | source)
XLA Modules:
  0.0 12.7 jit_solution(2462129133221091573)
XLA Ops:
  0.0 0.0 copy-start
  0.0 1.0 %copy-done = f32[5,2,64,128]{3,2,1,0:T(8,128)S(1)} copy-done((f32[5,2,64,128]{3,2,1,0:T(8,128)S(1)}, f32[5,2,64,128]{3,2,1,0:T(8,128)}, u32[]{:S(2)}) %copy-start) | copy-done | bytes 327704
  1.0 0.0 copy-start.2
  1.0 0.0 copy-start.4
  1.0 0.0 copy-start.5
  1.0 0.0 copy-start.6
  1.0 0.0 copy-start.9
  1.0 0.0 copy-start.10
  1.0 0.0 copy-start.11
  1.1 0.0 copy-start.7
  1.1 1.6 %collective-permute-start = (f32[96,128]{1,0:T(8,128)S(1)}, f32[96,128]{1,0:T(8,128)S(1)}, u32[]{:S(2)}, u32[]{:S(2)}) collective-permute-start(f32[96,128]{1,0:T(8,128)S(1)} %get-tuple-element.19), channel_id=1, source_target_pairs={{0,2},{1,3},{2,0},{3,1},{4,6},{5,7},{6,4},{7,5},{8,10},{9,11},{10,... | collective-permute-start | bytes 147464 | tf_op jit(solution)/shard_map/ppermute | solution.py:515
  2.7 0.0 copy-start.8
  2.7 0.0 collective-permute-start.1
  2.7 0.0 copy-done.2
  2.7 0.0 copy-done.3
  2.7 0.0 copy-done.4
  2.7 0.0 copy-done.5
  2.7 0.0 copy-done.6
  2.8 0.0 copy-done.9
  2.8 0.0 copy-done.10
  2.8 0.0 copy-done.11
  2.8 0.0 copy-done.7
  2.8 0.6 %copy-done.8 = f32[4,5,2]{1,2,0:T(2,128)S(1)} copy-done((f32[4,5,2]{1,2,0:T(2,128)S(1)}, f32[4,5,2]{1,2,0:T(2,128)}, u32[]{:S(2)}) %copy-start.8) | copy-done | bytes 184
  3.4 1.2 %prepare.1 = (f32[5,2,80,128]{3,2,1,0:T(8,128)S(1)}, f32[80,128]{1,0:T(8,128)S(1)}, f32[80,128]{1,0:T(8,128)S(1)}, f32[80,128]{1,0:T(8,128)S(1)}, f32[2,32,8,128...) custom-call(f32[5,2,64,128]{3,2,1,0:T(8,128)S(1)} %copy-done, ...), custom_call_target="tpu_custom_call" | custom-call | tf_op jit(solution)/shard_map/prepare/pallas_call | solution.py:496
  4.6 0.6 %collective-permute-done.first_round = f32[96,128]{1,0:T(8,128)S(1)} collective-permute-done((f32[96,128]{1,0:T(8,128)S(1)}, f32[96,128]{1,0:T(8,128)S(1)}, u32[]{:S(2)}, u32[]{:S(2)}) %collective-permute-start) | collective-permute-done | bytes 49184 | tf_op jit(solution)/shard_map/ppermute | solution.py:515
  5.2 1.6 %collective-permute-done.1.second_round = f32[96,128]{1,0:T(8,128)S(1)} collective-permute-done((f32[96,128]{1,0:T(8,128)S(1)}, f32[96,128]{1,0:T(8,128)S(1)}, u32[]{:S(2)}, u32[]{:S(2)}) %collective-permute-start.1) | collective-permute-done | bytes 49184 | tf_op jit(solution)/shard_map/ppermute | solution.py:516
  6.8 0.1 pack_x.1.refs_1_
  6.9 0.6 %collective-permute-start.2 = (f32[96,128]{1,0:T(8,128)S(1)}, f32[96,128]{1,0:T(8,128)S(1)}, u32[]{:S(2)}, u32[]{:S(2)}) collective-permute-start(f32[96,128]{1,0:T(8,128)S(1)} %pack_x.1.refs_1_), channel_id=1, source_target_pairs={{0,1},{1,0},{2,3},{3,2},{4,5},{5,4},{6,7},{7,6},{8,9},{9,8},{10,11... | collective-permute-start | bytes 147464 | tf_op jit(solution)/shard_map/ppermute | solution.py:557
  7.5 0.0 copy-done.1
  7.5 2.1 %begin.1 = (f32[5,2,64,128]{3,2,1,0:T(8,128)S(1)}, f32[3,80,128]{2,1,0:T(8,128)S(1)}) custom-call(f32[5,2,64,128]{3,2,1,0:T(8,128)S(1)} %copy-done.1, f32[96,128]{1,0:T(8,128)S(1)} %collective-permute-done.first_round, f32[96,128]{1,0:T(8,128)S(1)} %collective-permute-done.1.second_round, f32[5,2,80,128]{3,2,1,0:T(8,128)S(1)} %get-tuple-element.22.drive, ...), custom_call_target="tpu_custom_call" | custom-call | tf_op jit(solution)/shard_map/begin/pallas_call | solution.py:496
  9.6 1.5 %collective-permute-done.2.refs_0_ = f32[96,128]{1,0:T(8,128)S(1)} collective-permute-done((f32[96,128]{1,0:T(8,128)S(1)}, f32[96,128]{1,0:T(8,128)S(1)}, u32[]{:S(2)}, u32[]{:S(2)}) %collective-permute-start.2) | collective-permute-done | bytes 49184 | tf_op jit(solution)/shard_map/ppermute | solution.py:557
  11.1 1.6 %finish.1 = f32[5,2,64,128]{3,2,1,0:T(8,128)} custom-call(f32[96,128]{1,0:T(8,128)S(1)} %collective-permute-done.2.refs_0_, f32[96,128]{1,0:T(8,128)S(1)} %pack_x.1.refs_1_, f32[3,80,128]{2,1,0:T(8,128)S(1)} %get-tuple-element.26.refs_2_, f32[2,80,128]{2,1,0:T(8,128)S(1)} %get-tuple-element.27.refs_3_, bf16[384,256]{1,0:T(8,128)(2,1)S(1)} %get-tuple-element.28.refs_4_, ...), custom_call_target="tpu_custom_call" | custom-call | tf_op jit(solution)/shard_map/finish/pallas_call | solution.py:496
  (3 shorter events, 0.0 us)
Async XLA Ops:
  0.0 1.0 %copy-start = (f32[5,2,64,128]{3,2,1,0:T(8,128)S(1)}, f32[5,2,64,128]{3,2,1,0:T(8,128)}, u32[]{:S(2)}) copy-start(f32[5,2,64,128]{3,2,1,0:T(8,128)} %fields.5) | copy-start | bytes 983044
  1.0 1.7 %copy-start.2 = (bf16[2,128,128]{2,1,0:T(8,128)(2,1)S(1)}, bf16[2,128,128]{2,1,0:T(8,128)(2,1)}, u32[]{:S(2)}) copy-start(bf16[2,128,128]{2,1,0:T(8,128)(2,1)} %constant.2.clone.own_band) | copy-start | bytes 196612
  1.0 1.7 %copy-start.3 = (bf16[5,2,8,256]{3,2,1,0:T(8,128)(2,1)S(1)}, bf16[5,2,8,256]{3,2,1,0:T(8,128)(2,1)}, u32[]{:S(2)}) copy-start(bf16[5,2,8,256]{3,2,1,0:T(8,128)(2,1)} %north.1) | copy-start | bytes 122884
  1.0 1.8 %copy-start.4 = (bf16[5,2,8,256]{3,2,1,0:T(8,128)(2,1)S(1)}, bf16[5,2,8,256]{3,2,1,0:T(8,128)(2,1)}, u32[]{:S(2)}) copy-start(bf16[5,2,8,256]{3,2,1,0:T(8,128)(2,1)} %south.1) | copy-start | bytes 122884
  1.0 1.8 %copy-start.5 = (bf16[5,2,256,8]{2,3,1,0:T(8,128)(2,1)S(1)}, bf16[5,2,256,8]{2,3,1,0:T(8,128)(2,1)}, u32[]{:S(2)}) copy-start(bf16[5,2,256,8]{2,3,1,0:T(8,128)(2,1)} %param.17) | copy-start | bytes 122884
  1.0 1.8 %copy-start.6 = (bf16[5,2,256,8]{2,3,1,0:T(8,128)(2,1)S(1)}, bf16[5,2,256,8]{2,3,1,0:T(8,128)(2,1)}, u32[]{:S(2)}) copy-start(bf16[5,2,256,8]{2,3,1,0:T(8,128)(2,1)} %param.18) | copy-start | bytes 122884
  1.0 1.8 %copy-start.9 = (s32[4]{0:T(128)S(1)}, s32[4]{0:T(128)}, u32[]{:S(2)}) copy-start(s32[4]{0:T(128)} %widths.1) | copy-start | bytes 52
  1.0 1.8 %copy-start.10 = (f32[2]{0:T(128)S(1)}, f32[2]{0:T(128)}, u32[]{:S(2)}) copy-start(f32[2]{0:T(128)} %wind_x.1) | copy-start | bytes 28
  1.0 1.8 %copy-start.11 = (f32[2]{0:T(128)S(1)}, f32[2]{0:T(128)}, u32[]{:S(2)}) copy-start(f32[2]{0:T(128)} %wind_y.1) | copy-start | bytes 28
  1.1 1.7 %copy-start.7 = (f32[2,5,5]{2,0,1:T(2,128)S(1)}, f32[2,5,5]{2,0,1:T(2,128)}, u32[]{:S(2)}) copy-start(f32[2,5,5]{2,0,1:T(2,128)} %param.14) | copy-start | bytes 604
  1.1 4.2 %collective-permute-start = (f32[96,128]{1,0:T(8,128)S(1)}, f32[96,128]{1,0:T(8,128)S(1)}, u32[]{:S(2)}, u32[]{:S(2)}) collective-permute-start(f32[96,128]{1,0:T(8,128)S(1)} %get-tuple-element.19), channel_id=1, source_target_pairs={{0,2},{1,3},{2,0},{3,1},{4,6},{5,7},{6,4},{7,5},{8,10},{9,11},{10,... | collective-permute-start | bytes 147464 | tf_op jit(solution)/shard_map/ppermute | solution.py:515
  2.7 0.7 %copy-start.8 = (f32[4,5,2]{1,2,0:T(2,128)S(1)}, f32[4,5,2]{1,2,0:T(2,128)}, u32[]{:S(2)}) copy-start(f32[4,5,2]{1,2,0:T(2,128)} %param.19) | copy-start | bytes 484
  2.7 4.1 %collective-permute-start.1 = (f32[96,128]{1,0:T(8,128)S(1)}, f32[96,128]{1,0:T(8,128)S(1)}, u32[]{:S(2)}, u32[]{:S(2)}) collective-permute-start(f32[96,128]{1,0:T(8,128)S(1)} %get-tuple-element.20), channel_id=1, source_target_pairs={{0,8},{1,9},{2,4},{3,5},{4,2},{5,3},{6,14},{7,15},{8,0},{9,1},{10,... | collective-permute-start | bytes 147464 | tf_op jit(solution)/shard_map/ppermute | solution.py:516
  3.4 4.1 %copy-start.1 = (f32[5,2,64,128]{3,2,1,0:T(8,128)S(1)}, f32[5,2,64,128]{3,2,1,0:T(8,128)}, u32[]{:S(2)}) copy-start(f32[5,2,64,128]{3,2,1,0:T(8,128)} %fields.5) | copy-start | bytes 983044
  6.9 4.2 %collective-permute-start.2 = (f32[96,128]{1,0:T(8,128)S(1)}, f32[96,128]{1,0:T(8,128)S(1)}, u32[]{:S(2)}, u32[]{:S(2)}) collective-permute-start(f32[96,128]{1,0:T(8,128)S(1)} %pack_x.1.refs_1_), channel_id=1, source_target_pairs={{0,1},{1,0},{2,3},{3,2},{4,5},{5,4},{6,7},{7,6},{8,9},{9,8},{10,11... | collective-permute-start | bytes 147464 | tf_op jit(solution)/shard_map/ppermute | solution.py:557

commit v2 on v1

--- a/solution.py
+++ b/solution.py
@@ -258,28 +258,44 @@
                     ref[part, at : at + strip, :] = value[part]
 
 
+def corner_slot(index, count, rows):
+    planes = rows // PAD
+    return HALO * (count + index // planes), PAD * (index % planes)
+
+
 def pack_x_kernel(grid_sizes, first_round, second_round, *rest):
     gy_count, gx_count = grid_sizes
-    sides = (len(rest) - 1) // 2
-    payloads, outs, ext = rest[:sides], rest[sides:-1], rest[-1]
+    sides = (len(rest) - 1) // 3
+    payloads, outs, edges, ext = rest[:sides], rest[sides : 2 * sides], rest[2 * sides : -1], rest[-1]
     cols = first_round.shape[1]
     rows = payloads[0].shape[0]
+    count = ext.shape[0]
     lane = iota((2 * PAD, LANES), 1)
     starts = sent_starts(gx_count, cols)
     packed = [jnp.zeros((2 * PAD, LANES), jnp.float32) for _ in starts]
     ext[...] = jnp.zeros_like(ext)
-    for index in range(ext.shape[0]):
+    blocks = [
+        [payload[row : row + PAD, :] for row in range(0, rows, PAD)] for payload in payloads
+    ]
+    for index in range(count):
         slot = index * HALO
+        corner, row = corner_slot(index, count, rows)
         north, south = halo_rows(gy_count, first_round, second_round, slot)
         ext[index, PAD - HALO : PAD, 0:cols] = north
         ext[index, PAD : PAD + HALO, 0:cols] = south
         for n, start in enumerate(starts):
             moved = pltpu.roll(ext[index], lax.rem(slot + LANES - start, LANES), 1)
             packed[n] = jnp.where((lane >= slot) & (lane < slot + HALO), moved, packed[n])
-    for out, payload, value in zip(outs, payloads, packed):
-        out[0:PAD, :] = value[0:PAD]
-        out[PAD : PAD + rows, :] = payload[...]
-        out[PAD + rows : 2 * PAD + rows, :] = value[PAD : 2 * PAD]
+            near = ext[index, FIRST : FIRST + PAD, :]
+            moved = pltpu.roll(near, lax.rem(corner + LANES - start, LANES), 1)
+            here = (lane[0:PAD] >= corner) & (lane[0:PAD] < corner + HALO)
+            blocks[n][row // PAD] = jnp.where(here, moved, blocks[n][row // PAD])
+    for n, payload in enumerate(payloads):
+        for block, value in enumerate(blocks[n]):
+            outs[n][block * PAD : (block + 1) * PAD, :] = value
+        edges[n][0:PAD, :] = packed[n][0:PAD]
+        edges[n][PAD : PAD + rows, :] = payload[...]
+        edges[n][PAD + rows : 2 * PAD + rows, :] = packed[n][PAD : 2 * PAD]
 
 
 def loaded(weights, l, fac, count_f):
@@ -394,7 +410,7 @@
     halos, edges, fars, side_drive, side_matrix = (
         refs[n * sides : (n + 1) * sides] for n in range(5)
     )
-    after, row_relax, inside, lane_weights, out, one, two, xdiv = refs[5 * sides :]
+    after, row_relax, inside, lane_weights, out, outer, one, two = refs[5 * sides :]
     count_f, count_l, rows, cols = out.shape
     wide_rows = row_relax.shape[0]
     gx = lax.axis_index("gx")
@@ -404,6 +420,22 @@
     mix = [lane_weights[2 * REACH + d] for d in range(2 * count_f - 1)]
     speed = lane_weights[lane_weights.shape[0] - 1]
 
+    def unpack(halo):
+        count = count_f * count_l
+        outer[0:8, :] = jnp.zeros((8, LANES), jnp.float32)
+        outer[PAD + rows + 8 : 2 * PAD + rows, :] = jnp.zeros((8, LANES), jnp.float32)
+        lane = iota((rows, LANES), 1)
+        outer[PAD : PAD + rows, :] = jnp.where(lane < HALO * count, halo[...], 0.0)
+        lane = iota((PAD, LANES), 1)
+        corners = jnp.zeros((PAD, LANES), jnp.float32)
+        for index in range(count):
+            slot = HALO * index
+            corner, row = corner_slot(index, count, rows)
+            moved = pltpu.roll(halo[row : row + PAD, :], (slot - corner) % LANES, 1)
+            corners = jnp.where((lane >= slot) & (lane < slot + HALO), moved, corners)
+        outer[8:PAD, :] = corners[0:8]
+        outer[PAD + rows : PAD + rows + 8, :] = corners[8:PAD]
+
     def section(parts, s, fac, number, first, height, wanted, store):
         columns = [part[first : first + height, :] for part in parts]
         columns.append(fars[s][number, first - FIRST : first - FIRST + height, :])
@@ -411,23 +443,28 @@
         moved = jnp.dot(
             both, side_matrix[s][:, wanted[0] * LANES :], preferred_element_type=jnp.float32
         )
-        moved = moved[0:height] + moved[height:]
-        for n, which in enumerate(wanted):
-            xdiv[which, 0:height, :] = moved[:, n * LANES : (n + 1) * LANES]
+        rates = {}
         for which in wanted:
-            part, start = parts[which], (halos, edges)[which][s]
+            part = parts[which]
             for n in range(height // 8):
-                at, row = first + n * 8, n * 8
+                at = first + n * 8
                 to = at - FIRST
                 center = part[at : at + 8, :]
-                rate = side_drive[s][which, to : to + 8, :] + speed * xdiv[which, row : row + 8, :]
-                rate = rate - row_relax[to : to + 8, :] * center
+                rate = side_drive[s][which, to : to + 8, :] - row_relax[to : to + 8, :] * center
+                rate = y_terms(lambda row: part[row : row + 8, :], at, taps, rate)
                 for d, entry in enumerate(mix):
                     step = (d - (count_f - 1)) * HALO * count_l
                     other = pltpu.roll(center, -step % LANES, 1) if step else center
                     rate = rate + entry * other
-                rate = y_terms(lambda row: part[row : row + 8, :], at, taps, rate)
-                store(which, at, to, start[at : at + 8, :] + fac * rate)
+                rates[which, n] = rate
+        for place, which in enumerate(wanted):
+            start = (outer, edges[s])[which]
+            lanes = slice(place * LANES, (place + 1) * LANES)
+            for n in range(height // 8):
+                at, row = first + n * 8, n * 8
+                x_rate = moved[row : row + 8, lanes] + moved[height + row : height + row + 8, lanes]
+                rate = rates[which, n] + speed * x_rate
+                store(which, at, at - FIRST, start[at : at + 8, :] + fac * rate)
 
     lane = iota((rows, LANES), 1)
     for s in range(sides):
@@ -440,7 +477,8 @@
 
             return store
 
-        section((halos[s], edges[s]), s, THIRD, 0, FIRST, wide_rows, (0, 1), keep(one))
+        unpack(halos[s])
+        section((outer, edges[s]), s, THIRD, 0, FIRST, wide_rows, (0, 1), keep(one))
         section((one.at[0], one.at[1]), s, HALF, 1, FIRST, wide_rows, (0, 1), keep(two))
 
         def last(which, at, to, value):
@@ -544,13 +582,14 @@
         prepared[7 + n * sides : 7 + (n + 1) * sides] for n in range(3)
     )
 
-    sent = call(
+    packed_x = call(
         functools.partial(pack_x_kernel, grid_sizes),
         "pack_x",
-        (f32((ext_rows, LANES)),) * sides,
+        (f32((rows, LANES)),) * sides + (f32((ext_rows, LANES)),) * sides,
         inputs(vmem, first_round, second_round, *payloads),
         scratch=[pltpu.VMEM((count_f * count_l, 2 * PAD, LANES), jnp.float32)],
     )
+    sent, edges = packed_x[:sides], packed_x[sides:]
     forward = [(i, i + 1) for i in range(gx_count - 1)]
     backward = [(b, a) for a, b in forward]
     if sides == 1:
@@ -572,9 +611,9 @@
         functools.partial(finish_kernel, grid_sizes, sides),
         "finish",
         f32(fields.shape),
-        inputs(vmem, *halos, *sent[::-1], *far, *side_drive, *side_matrix)
+        inputs(vmem, *halos, *edges[::-1], *far, *side_drive, *side_matrix)
         + inputs(vmem, after, row_relax, inside, lane_weights),
-        scratch=[pair, pair, pltpu.VMEM((2, wide_rows, LANES), jnp.float32)],
+        scratch=[pltpu.VMEM((ext_rows, LANES), jnp.float32), pair, pair],
     )
 
 

time: 12.9 us -> 12.6 us (0.977)
  the two profiles are of different devices: /device:TPU:18 before, /device:TPU:16 now
where the time goes in v2:
time: 12.6 us; the launch traced here: 12.5 us
  Pallas kernels  5.01 us (40%)
  starting transfers between devices  3.2 us (25%)
  waiting for transfers between devices  2.5 us (20%)
  local copies, waits for them, and re-layouts  1.62 us (13%)
  between operations  0.14 us (1%)
    pallas_call x5, Pallas kernels, call(): pl.pallas_call(body, out_shape=out_shape, in_specs=[space for _, space in...  5.01 us
    ppermute x1, starting transfers between devices, local(): first_round = lax.ppermute(sent_first, axes, first_pairs)  1.64 us
    unnamed x24, local copies, waits for them, and re-layouts  1.62 us
    ppermute x1, waiting for transfers between devices, local(): second_round = lax.ppermute(sent_second, axes, second_pairs)  1.58 us
    ppermute x1, starting transfers between devices, local(): halos = [lax.ppermute(sent[0], 'gx', forward + backward)]  1.56 us
    ppermute x1, waiting for transfers between devices, local(): first_round = lax.ppermute(sent_first, axes, first_pairs)  0.6 us
    ppermute x1, waiting for transfers between devices, local(): halos = [lax.ppermute(sent[0], 'gx', forward + backward)]  0.32 us
  transfers between devices with their start and end apart: 3, of which 3 were waited for; matrix products, arithmetic and copies ran while one was open for 0% of the time, Pallas kernels for 26%

profile of v2, /device:TPU:16, one launch (start us, length us, event | category | flops | bytes accessed | tf_op | source)
XLA Modules:
  0.0 12.5 jit_solution(18103996209976284921)
XLA Ops:
  0.0 0.0 copy-start
  0.0 1.0 %copy-done = f32[5,2,64,128]{3,2,1,0:T(8,128)S(1)} copy-done((f32[5,2,64,128]{3,2,1,0:T(8,128)S(1)}, f32[5,2,64,128]{3,2,1,0:T(8,128)}, u32[]{:S(2)}) %copy-start) | copy-done | bytes 327704
  1.0 0.0 copy-start.2
  1.0 0.0 copy-start.4
  1.0 0.0 copy-start.5
  1.0 0.0 copy-start.6
  1.0 0.0 copy-start.9
  1.0 0.0 copy-start.10
  1.0 0.0 copy-start.11
  1.1 0.0 copy-start.7
  1.1 1.6 %collective-permute-start = (f32[96,128]{1,0:T(8,128)S(1)}, f32[96,128]{1,0:T(8,128)S(1)}, u32[]{:S(2)}, u32[]{:S(2)}) collective-permute-start(f32[96,128]{1,0:T(8,128)S(1)} %get-tuple-element.21), channel_id=1, source_target_pairs={{0,2},{1,3},{2,0},{3,1},{4,6},{5,7},{6,4},{7,5},{8,10},{9,11},{10,... | collective-permute-start | bytes 147464 | tf_op jit(solution)/shard_map/ppermute | solution.py:553
  2.7 0.0 copy-start.8
  2.7 0.0 collective-permute-start.1
  2.7 0.0 copy-done.2
  2.7 0.0 copy-done.3
  2.7 0.0 copy-done.4
  2.7 0.0 copy-done.5
  2.7 0.0 copy-done.6
  2.8 0.0 copy-done.9
  2.8 0.0 copy-done.10
  2.8 0.0 copy-done.11
  2.8 0.0 copy-done.7
  2.8 0.6 %copy-done.8 = f32[4,5,2]{1,2,0:T(2,128)S(1)} copy-done((f32[4,5,2]{1,2,0:T(2,128)S(1)}, f32[4,5,2]{1,2,0:T(2,128)}, u32[]{:S(2)}) %copy-start.8) | copy-done | bytes 184
  3.4 1.2 %prepare.1 = (f32[5,2,80,128]{3,2,1,0:T(8,128)S(1)}, f32[80,128]{1,0:T(8,128)S(1)}, f32[80,128]{1,0:T(8,128)S(1)}, f32[80,128]{1,0:T(8,128)S(1)}, f32[2,32,8,128...) custom-call(f32[5,2,64,128]{3,2,1,0:T(8,128)S(1)} %copy-done, ...), custom_call_target="tpu_custom_call" | custom-call | tf_op jit(solution)/shard_map/prepare/pallas_call | solution.py:534
  4.6 0.6 %collective-permute-done.first_round = f32[96,128]{1,0:T(8,128)S(1)} collective-permute-done((f32[96,128]{1,0:T(8,128)S(1)}, f32[96,128]{1,0:T(8,128)S(1)}, u32[]{:S(2)}, u32[]{:S(2)}) %collective-permute-start) | collective-permute-done | bytes 49184 | tf_op jit(solution)/shard_map/ppermute | solution.py:553
  5.2 1.6 %collective-permute-done.1.second_round = f32[96,128]{1,0:T(8,128)S(1)} collective-permute-done((f32[96,128]{1,0:T(8,128)S(1)}, f32[96,128]{1,0:T(8,128)S(1)}, u32[]{:S(2)}, u32[]{:S(2)}) %collective-permute-start.1) | collective-permute-done | bytes 49184 | tf_op jit(solution)/shard_map/ppermute | solution.py:554
  6.8 0.1 %pack_x.1 = (f32[64,128]{1,0:T(8,128)S(1)}, f32[96,128]{1,0:T(8,128)S(1)}) custom-call(f32[96,128]{1,0:T(8,128)S(1)} %collective-permute-done.first_round, f32[96,128]{1,0:T(8,128)S(1)} %collective-permute-done.1.second_round, f32[64,128]{1,0:T(8,128)S(1)} %get-tuple-element.23.rest_0_), custom_call_target="tpu_custom_call" | custom-call | tf_op jit(solution)/shard_map/pack_x/pallas_call | solution.py:534
  7.0 1.6 %collective-permute-start.2 = (f32[64,128]{1,0:T(8,128)S(1)}, f32[64,128]{1,0:T(8,128)S(1)}, u32[]{:S(2)}, u32[]{:S(2)}) collective-permute-start(f32[64,128]{1,0:T(8,128)S(1)} %get-tuple-element.24), channel_id=1, source_target_pairs={{0,1},{1,0},{2,3},{3,2},{4,5},{5,4},{6,7},{7,6},{8,9},{9,8},{10,11... | collective-permute-start | bytes 98312 | tf_op jit(solution)/shard_map/ppermute | solution.py:596
  8.5 0.0 copy-done.1
  8.5 2.1 %begin.1 = (f32[5,2,64,128]{3,2,1,0:T(8,128)S(1)}, f32[3,80,128]{2,1,0:T(8,128)S(1)}) custom-call(f32[5,2,64,128]{3,2,1,0:T(8,128)S(1)} %copy-done.1, f32[96,128]{1,0:T(8,128)S(1)} %collective-permute-done.first_round, f32[96,128]{1,0:T(8,128)S(1)} %collective-permute-done.1.second_round, f32[5,2,80,128]{3,2,1,0:T(8,128)S(1)} %get-tuple-element.26.drive, ...), custom_call_target="tpu_custom_call" | custom-call | tf_op jit(solution)/shard_map/begin/pallas_call | solution.py:534
  10.6 0.3 %collective-permute-done.2.refs_0_ = f32[64,128]{1,0:T(8,128)S(1)} collective-permute-done((f32[64,128]{1,0:T(8,128)S(1)}, f32[64,128]{1,0:T(8,128)S(1)}, u32[]{:S(2)}, u32[]{:S(2)}) %collective-permute-start.2) | collective-permute-done | bytes 32800 | tf_op jit(solution)/shard_map/ppermute | solution.py:596
  10.9 1.5 %finish.1 = f32[5,2,64,128]{3,2,1,0:T(8,128)} custom-call(f32[64,128]{1,0:T(8,128)S(1)} %collective-permute-done.2.refs_0_, f32[96,128]{1,0:T(8,128)S(1)} %get-tuple-element.25.refs_1_, f32[3,80,128]{2,1,0:T(8,128)S(1)} %get-tuple-element.30.refs_2_, f32[2,80,128]{2,1,0:T(8,128)S(1)} %get-tuple-element.31.refs_3_, ...), custom_call_target="tpu_custom_call" | custom-call | tf_op jit(solution)/shard_map/finish/pallas_call | solution.py:534
  (3 shorter events, 0.0 us)
Async XLA Ops:
  0.0 1.0 %copy-start = (f32[5,2,64,128]{3,2,1,0:T(8,128)S(1)}, f32[5,2,64,128]{3,2,1,0:T(8,128)}, u32[]{:S(2)}) copy-start(f32[5,2,64,128]{3,2,1,0:T(8,128)} %fields.5) | copy-start | bytes 983044
  1.0 1.7 %copy-start.2 = (bf16[2,128,128]{2,1,0:T(8,128)(2,1)S(1)}, bf16[2,128,128]{2,1,0:T(8,128)(2,1)}, u32[]{:S(2)}) copy-start(bf16[2,128,128]{2,1,0:T(8,128)(2,1)} %constant.2.clone.own_band) | copy-start | bytes 196612
  1.0 1.7 %copy-start.3 = (bf16[5,2,8,256]{3,2,1,0:T(8,128)(2,1)S(1)}, bf16[5,2,8,256]{3,2,1,0:T(8,128)(2,1)}, u32[]{:S(2)}) copy-start(bf16[5,2,8,256]{3,2,1,0:T(8,128)(2,1)} %north.1) | copy-start | bytes 122884
  1.0 1.8 %copy-start.4 = (bf16[5,2,8,256]{3,2,1,0:T(8,128)(2,1)S(1)}, bf16[5,2,8,256]{3,2,1,0:T(8,128)(2,1)}, u32[]{:S(2)}) copy-start(bf16[5,2,8,256]{3,2,1,0:T(8,128)(2,1)} %south.1) | copy-start | bytes 122884
  1.0 1.8 %copy-start.5 = (bf16[5,2,256,8]{2,3,1,0:T(8,128)(2,1)S(1)}, bf16[5,2,256,8]{2,3,1,0:T(8,128)(2,1)}, u32[]{:S(2)}) copy-start(bf16[5,2,256,8]{2,3,1,0:T(8,128)(2,1)} %param.17) | copy-start | bytes 122884
  1.0 1.8 %copy-start.6 = (bf16[5,2,256,8]{2,3,1,0:T(8,128)(2,1)S(1)}, bf16[5,2,256,8]{2,3,1,0:T(8,128)(2,1)}, u32[]{:S(2)}) copy-start(bf16[5,2,256,8]{2,3,1,0:T(8,128)(2,1)} %param.18) | copy-start | bytes 122884
  1.0 1.8 %copy-start.9 = (s32[4]{0:T(128)S(1)}, s32[4]{0:T(128)}, u32[]{:S(2)}) copy-start(s32[4]{0:T(128)} %widths.1) | copy-start | bytes 52
  1.0 1.8 %copy-start.10 = (f32[2]{0:T(128)S(1)}, f32[2]{0:T(128)}, u32[]{:S(2)}) copy-start(f32[2]{0:T(128)} %wind_x.1) | copy-start | bytes 28
  1.0 1.8 %copy-start.11 = (f32[2]{0:T(128)S(1)}, f32[2]{0:T(128)}, u32[]{:S(2)}) copy-start(f32[2]{0:T(128)} %wind_y.1) | copy-start | bytes 28
  1.1 1.7 %copy-start.7 = (f32[2,5,5]{2,0,1:T(2,128)S(1)}, f32[2,5,5]{2,0,1:T(2,128)}, u32[]{:S(2)}) copy-start(f32[2,5,5]{2,0,1:T(2,128)} %param.14) | copy-start | bytes 604
  1.1 4.2 %collective-permute-start = (f32[96,128]{1,0:T(8,128)S(1)}, f32[96,128]{1,0:T(8,128)S(1)}, u32[]{:S(2)}, u32[]{:S(2)}) collective-permute-start(f32[96,128]{1,0:T(8,128)S(1)} %get-tuple-element.21), channel_id=1, source_target_pairs={{0,2},{1,3},{2,0},{3,1},{4,6},{5,7},{6,4},{7,5},{8,10},{9,11},{10,... | collective-permute-start | bytes 147464 | tf_op jit(solution)/shard_map/ppermute | solution.py:553
  2.7 0.7 %copy-start.8 = (f32[4,5,2]{1,2,0:T(2,128)S(1)}, f32[4,5,2]{1,2,0:T(2,128)}, u32[]{:S(2)}) copy-start(f32[4,5,2]{1,2,0:T(2,128)} %param.19) | copy-start | bytes 484
  2.7 4.1 %collective-permute-start.1 = (f32[96,128]{1,0:T(8,128)S(1)}, f32[96,128]{1,0:T(8,128)S(1)}, u32[]{:S(2)}, u32[]{:S(2)}) collective-permute-start(f32[96,128]{1,0:T(8,128)S(1)} %get-tuple-element.22), channel_id=1, source_target_pairs={{0,8},{1,9},{2,4},{3,5},{4,2},{5,3},{6,14},{7,15},{8,0},{9,1},{10,... | collective-permute-start | bytes 147464 | tf_op jit(solution)/shard_map/ppermute | solution.py:554
  3.4 5.1 %copy-start.1 = (f32[5,2,64,128]{3,2,1,0:T(8,128)S(1)}, f32[5,2,64,128]{3,2,1,0:T(8,128)}, u32[]{:S(2)}) copy-start(f32[5,2,64,128]{3,2,1,0:T(8,128)} %fields.5) | copy-start | bytes 983044
  7.0 4.0 %collective-permute-start.2 = (f32[64,128]{1,0:T(8,128)S(1)}, f32[64,128]{1,0:T(8,128)S(1)}, u32[]{:S(2)}, u32[]{:S(2)}) collective-permute-start(f32[64,128]{1,0:T(8,128)S(1)} %get-tuple-element.24), channel_id=1, source_target_pairs={{0,1},{1,0},{2,3},{3,2},{4,5},{5,4},{6,7},{7,6},{8,9},{9,8},{10,11... | collective-permute-start | bytes 98312 | tf_op jit(solution)/shard_map/ppermute | solution.py:596

commit v3 on v2

--- a/solution.py
+++ b/solution.py
@@ -331,6 +331,19 @@
     xdiv[:, 0:height, :] = moved.reshape(count_f, height, LANES)
 
 
+def packed_rate(part, at, forced, row_relax, lane_weights, count_f, count_l):
+    to = at - FIRST
+    center = part[at : at + 8, :]
+    rate = forced - row_relax[to : to + 8, :] * center
+    taps = [lane_weights[k] for k in range(2 * REACH)]
+    rate = y_terms(lambda row: part[row : row + 8, :], at, taps, rate)
+    for d in range(2 * count_f - 1):
+        step = (d - (count_f - 1)) * HALO * count_l
+        other = pltpu.roll(center, -step % LANES, 1) if step else center
+        rate = rate + lane_weights[2 * REACH + d] * other
+    return rate
+
+
 def begin_kernel(
     grid_sizes,
     fields,
@@ -340,11 +353,15 @@
     relax,
     weights,
     own_matrix,
-    after,
+    row_relax,
+    lane_weights,
     *rest,
 ):
     gy_count, gx_count = grid_sizes
-    far, (state, own_one, own_two, xdiv) = rest[:-4], rest[-4:]
+    sides = (len(rest) - 5) // 4
+    edges, side_drive, after = rest[:sides], rest[sides : 2 * sides], rest[2 * sides]
+    far, edge_one = rest[2 * sides + 1 : 3 * sides + 1], rest[3 * sides + 1 : -4]
+    state, own_one, own_two, xdiv = rest[-4:]
     count_f, count_l, rows, cols = fields.shape
     wide_rows = relax.shape[0]
     gy = lax.axis_index("gy")
@@ -372,6 +389,10 @@
             ref[section] = packed
 
     keep_far(state, 0)
+    for edge, forced, ref in zip(edges, side_drive, edge_one):
+        for to in range(0, wide_rows, 8):
+            rate = packed_rate(edge, FIRST + to, forced[1, to : to + 8, :], row_relax, lane_weights, count_f, count_l)
+            ref[to : to + 8, :] = edge[FIRST + to : FIRST + to + 8, :] + THIRD * rate
     for section, (src, dst, fac) in enumerate(
         ((state, own_one, THIRD), (own_one, own_two, HALF), (own_two, after, 1.0))
     ):
@@ -407,17 +428,15 @@
 
 def finish_kernel(grid_sizes, sides, *refs):
     gy_count, gx_count = grid_sizes
-    halos, edges, fars, side_drive, side_matrix = (
-        refs[n * sides : (n + 1) * sides] for n in range(5)
-    )
-    after, row_relax, inside, lane_weights, out, outer, one, two = refs[5 * sides :]
+    halos, edges, fars, edge_one, side_drive, side_matrix = (
+        refs[n * sides : (n + 1) * sides] for n in range(6)
+    )
+    after, row_relax, inside, lane_weights, out, outer, one, two = refs[6 * sides :]
     count_f, count_l, rows, cols = out.shape
     wide_rows = row_relax.shape[0]
     gx = lax.axis_index("gx")
     starts = edge_starts(gx_count, cols)[0]
     exists = [None] if sides == 1 else [gx > 0, gx < gx_count - 1]
-    taps = [lane_weights[k] for k in range(2 * REACH)]
-    mix = [lane_weights[2 * REACH + d] for d in range(2 * count_f - 1)]
     speed = lane_weights[lane_weights.shape[0] - 1]
 
     def unpack(halo):
@@ -439,32 +458,32 @@
     def section(parts, s, fac, number, first, height, wanted, store):
         columns = [part[first : first + height, :] for part in parts]
         columns.append(fars[s][number, first - FIRST : first - FIRST + height, :])
-        both = jnp.concatenate(split(jnp.concatenate(columns, axis=1)), axis=0)
+        both = jnp.concatenate(split(jnp.concatenate(columns, axis=1)), axis=1)
+        matrix = side_matrix[s][:, wanted[0] * LANES :]
         moved = jnp.dot(
-            both, side_matrix[s][:, wanted[0] * LANES :], preferred_element_type=jnp.float32
+            both, jnp.concatenate([matrix, matrix], axis=0), preferred_element_type=jnp.float32
         )
-        rates = {}
-        for which in wanted:
-            part = parts[which]
-            for n in range(height // 8):
+        places = []
+        for place, which in enumerate(wanted):
+            short = number == 1 and which == 0
+            for n in range(short, height // 8 - short):
                 at = first + n * 8
-                to = at - FIRST
-                center = part[at : at + 8, :]
-                rate = side_drive[s][which, to : to + 8, :] - row_relax[to : to + 8, :] * center
-                rate = y_terms(lambda row: part[row : row + 8, :], at, taps, rate)
-                for d, entry in enumerate(mix):
-                    step = (d - (count_f - 1)) * HALO * count_l
-                    other = pltpu.roll(center, -step % LANES, 1) if step else center
-                    rate = rate + entry * other
-                rates[which, n] = rate
-        for place, which in enumerate(wanted):
-            start = (outer, edges[s])[which]
-            lanes = slice(place * LANES, (place + 1) * LANES)
-            for n in range(height // 8):
-                at, row = first + n * 8, n * 8
-                x_rate = moved[row : row + 8, lanes] + moved[height + row : height + row + 8, lanes]
-                rate = rates[which, n] + speed * x_rate
-                store(which, at, at - FIRST, start[at : at + 8, :] + fac * rate)
+                rate = None
+                if number > 0 or which == 0:
+                    forced = side_drive[s][which, at - FIRST : at - FIRST + 8, :]
+                    rate = packed_rate(
+                        parts[which], at, forced, row_relax, lane_weights, count_f, count_l
+                    )
+                places.append((place, which, n, at, rate))
+        for place, which, n, at, rate in places:
+            lanes, row = slice(place * LANES, (place + 1) * LANES), n * 8
+            x_rate = moved[row : row + 8, lanes]
+            if rate is None:
+                value = edge_one[s][row : row + 8, :] + fac * (speed * x_rate)
+            else:
+                start = (outer, edges[s])[which]
+                value = start[at : at + 8, :] + fac * (rate + speed * x_rate)
+            store(which, at, at - FIRST, value)
 
     lane = iota((rows, LANES), 1)
     for s in range(sides):
@@ -598,11 +617,13 @@
         halos = [lax.ppermute(sent[0], "gx", forward), lax.ppermute(sent[1], "gx", backward)]
 
     state = pltpu.VMEM(state_shape, jnp.float32)
-    after, *far = call(
+    edges = edges[::-1]
+    after, *begun = call(
         functools.partial(begin_kernel, grid_sizes),
         "begin",
-        (f32(fields.shape),) + (f32((3, wide_rows, LANES)),) * sides,
-        inputs(vmem, fields, first_round, second_round, drive, relax, weights, own_matrix),
+        (f32(fields.shape),) + (f32((3, wide_rows, LANES)),) * sides + (plane,) * sides,
+        inputs(vmem, fields, first_round, second_round, drive, relax, weights, own_matrix)
+        + inputs(vmem, row_relax, lane_weights, *edges, *side_drive),
         scratch=[state] * 3 + [pltpu.VMEM((count_f, wide_rows, LANES), jnp.float32)],
         limit=8,
     )
@@ -611,7 +632,7 @@
         functools.partial(finish_kernel, grid_sizes, sides),
         "finish",
         f32(fields.shape),
-        inputs(vmem, *halos, *edges[::-1], *far, *side_drive, *side_matrix)
+        inputs(vmem, *halos, *edges, *begun, *side_drive, *side_matrix)
         + inputs(vmem, after, row_relax, inside, lane_weights),
         scratch=[pltpu.VMEM((ext_rows, LANES), jnp.float32), pair, pair],
     )

time: 12.6 us -> 12.6 us (level)
  transfers between devices with their start and end apart: 3 -> 3, of which waited for: 3 -> 3; matrix products, arithmetic and copies ran while one was open for 0% -> 0% of each run, Pallas kernels for 26% -> 27%
where the time goes in v3:
time: 12.6 us; the launch traced here: 12.5 us
  Pallas kernels  5.01 us (40%)
  starting transfers between devices  3.2 us (25%)
  waiting for transfers between devices  2.49 us (20%)
  local copies, waits for them, and re-layouts  1.62 us (13%)
  between operations  0.14 us (1%)
    pallas_call x5, Pallas kernels, call(): pl.pallas_call(body, out_shape=out_shape, in_specs=[space for _, space in...  5.01 us
    ppermute x1, starting transfers between devices, local(): first_round = lax.ppermute(sent_first, axes, first_pairs)  1.64 us
    unnamed x24, local copies, waits for them, and re-layouts  1.62 us
    ppermute x1, waiting for transfers between devices, local(): second_round = lax.ppermute(sent_second, axes, second_pairs)  1.58 us
    ppermute x1, starting transfers between devices, local(): halos = [lax.ppermute(sent[0], 'gx', forward + backward)]  1.56 us
    ppermute x1, waiting for transfers between devices, local(): first_round = lax.ppermute(sent_first, axes, first_pairs)  0.6 us
    ppermute x1, waiting for transfers between devices, local(): halos = [lax.ppermute(sent[0], 'gx', forward + backward)]  0.31 us
  transfers between devices with their start and end apart: 3, of which 3 were waited for; matrix products, arithmetic and copies ran while one was open for 0% of the time, Pallas kernels for 27%

profile of v3, /device:TPU:16, one launch (start us, length us, event | category | flops | bytes accessed | tf_op | source)
XLA Modules:
  0.0 12.5 jit_solution(3303224449468806510)
XLA Ops:
  0.0 0.0 copy-start
  0.0 1.0 %copy-done = f32[5,2,64,128]{3,2,1,0:T(8,128)S(1)} copy-done((f32[5,2,64,128]{3,2,1,0:T(8,128)S(1)}, f32[5,2,64,128]{3,2,1,0:T(8,128)}, u32[]{:S(2)}) %copy-start) | copy-done | bytes 327704
  1.0 0.0 copy-start.2
  1.0 0.0 copy-start.3
  1.0 0.0 copy-start.4
  1.0 0.0 copy-start.5
  1.0 0.0 copy-start.6
  1.0 0.0 copy-start.9
  1.0 0.0 copy-start.10
  1.0 0.0 copy-start.11
  1.1 0.0 copy-start.7
  1.1 1.6 %collective-permute-start = (f32[96,128]{1,0:T(8,128)S(1)}, f32[96,128]{1,0:T(8,128)S(1)}, u32[]{:S(2)}, u32[]{:S(2)}) collective-permute-start(f32[96,128]{1,0:T(8,128)S(1)} %get-tuple-element.22), channel_id=1, source_target_pairs={{0,2},{1,3},{2,0},{3,1},{4,6},{5,7},{6,4},{7,5},{8,10},{9,11},{10,... | collective-permute-start | bytes 147464 | tf_op jit(solution)/shard_map/ppermute | solution.py:572
  2.7 0.0 collective-permute-start.1
  2.7 0.0 copy-done.2
  2.7 0.0 copy-done.3
  2.7 0.0 copy-done.4
  2.7 0.0 copy-done.5
  2.7 0.0 copy-done.6
  2.8 0.0 copy-done.9
  2.8 0.0 copy-done.10
  2.8 0.0 copy-done.11
  2.8 0.0 copy-done.7
  2.8 0.6 %copy-done.8 = f32[4,5,2]{1,2,0:T(2,128)S(1)} copy-done((f32[4,5,2]{1,2,0:T(2,128)S(1)}, f32[4,5,2]{1,2,0:T(2,128)}, u32[]{:S(2)}) %copy-start.8) | copy-done | bytes 184
  3.4 1.2 %prepare.1 = (f32[5,2,80,128]{3,2,1,0:T(8,128)S(1)}, f32[80,128]{1,0:T(8,128)S(1)}, f32[80,128]{1,0:T(8,128)S(1)}, f32[80,128]{1,0:T(8,128)S(1)}, f32[2,32,8,128...) custom-call(f32[5,2,64,128]{3,2,1,0:T(8,128)S(1)} %copy-done, ...), custom_call_target="tpu_custom_call" | custom-call | tf_op jit(solution)/shard_map/prepare/pallas_call | solution.py:553
  4.6 0.6 %collective-permute-done.first_round = f32[96,128]{1,0:T(8,128)S(1)} collective-permute-done((f32[96,128]{1,0:T(8,128)S(1)}, f32[96,128]{1,0:T(8,128)S(1)}, u32[]{:S(2)}, u32[]{:S(2)}) %collective-permute-start) | collective-permute-done | bytes 49184 | tf_op jit(solution)/shard_map/ppermute | solution.py:572
  5.2 1.6 %collective-permute-done.1.second_round = f32[96,128]{1,0:T(8,128)S(1)} collective-permute-done((f32[96,128]{1,0:T(8,128)S(1)}, f32[96,128]{1,0:T(8,128)S(1)}, u32[]{:S(2)}, u32[]{:S(2)}) %collective-permute-start.1) | collective-permute-done | bytes 49184 | tf_op jit(solution)/shard_map/ppermute | solution.py:573
  6.8 0.1 %pack_x.1 = (f32[64,128]{1,0:T(8,128)S(1)}, f32[96,128]{1,0:T(8,128)S(1)}) custom-call(f32[96,128]{1,0:T(8,128)S(1)} %collective-permute-done.first_round, f32[96,128]{1,0:T(8,128)S(1)} %collective-permute-done.1.second_round, f32[64,128]{1,0:T(8,128)S(1)} %get-tuple-element.24.rest_0_), custom_call_target="tpu_custom_call" | custom-call | tf_op jit(solution)/shard_map/pack_x/pallas_call | solution.py:553
  7.0 1.6 %collective-permute-start.2 = (f32[64,128]{1,0:T(8,128)S(1)}, f32[64,128]{1,0:T(8,128)S(1)}, u32[]{:S(2)}, u32[]{:S(2)}) collective-permute-start(f32[64,128]{1,0:T(8,128)S(1)} %get-tuple-element.25), channel_id=1, source_target_pairs={{0,1},{1,0},{2,3},{3,2},{4,5},{5,4},{6,7},{7,6},{8,9},{9,8},{10,11... | collective-permute-start | bytes 98312 | tf_op jit(solution)/shard_map/ppermute | solution.py:615
  8.5 0.0 copy-done.1
  8.5 2.1 %begin.1 = (f32[5,2,64,128]{3,2,1,0:T(8,128)S(1)}, f32[3,80,128]{2,1,0:T(8,128)S(1)}, f32[80,128]{1,0:T(8,128)S(1)}) custom-call(f32[5,2,64,128]{3,2,1,0:T(8,128)S(1)} %copy-done.1, f32[96,128]{1,0:T(8,128)S(1)} %collective-permute-done.first_round, f32[96,128]{1,0:T(8,128)S(1)} %collective-permute-done.1.second_round, ...), custom_call_target="tpu_custom_call" | custom-call | tf_op jit(solution)/shard_map/begin/pallas_call | solution.py:553
  10.6 0.3 %collective-permute-done.2.refs_0_ = f32[64,128]{1,0:T(8,128)S(1)} collective-permute-done((f32[64,128]{1,0:T(8,128)S(1)}, f32[64,128]{1,0:T(8,128)S(1)}, u32[]{:S(2)}, u32[]{:S(2)}) %collective-permute-start.2) | collective-permute-done | bytes 32800 | tf_op jit(solution)/shard_map/ppermute | solution.py:615
  10.9 1.5 %finish.1 = f32[5,2,64,128]{3,2,1,0:T(8,128)} custom-call(f32[64,128]{1,0:T(8,128)S(1)} %collective-permute-done.2.refs_0_, f32[96,128]{1,0:T(8,128)S(1)} %get-tuple-element.26.rest_0_.refs_1_, f32[3,80,128]{2,1,0:T(8,128)S(1)} %get-tuple-element.34.refs_2_, f32[80,128]{1,0:T(8,128)S(1)} %get-tuple-element.35.refs_3_, ...), custom_call_target="tpu_custom_call" | custom-call | tf_op jit(solution)/shard_map/finish/pallas_call | solution.py:553
  (3 shorter events, 0.0 us)
Async XLA Ops:
  0.0 1.0 %copy-start = (f32[5,2,64,128]{3,2,1,0:T(8,128)S(1)}, f32[5,2,64,128]{3,2,1,0:T(8,128)}, u32[]{:S(2)}) copy-start(f32[5,2,64,128]{3,2,1,0:T(8,128)} %fields.5) | copy-start | bytes 983044
  1.0 1.7 %copy-start.2 = (bf16[2,128,128]{2,1,0:T(8,128)(2,1)S(1)}, bf16[2,128,128]{2,1,0:T(8,128)(2,1)}, u32[]{:S(2)}) copy-start(bf16[2,128,128]{2,1,0:T(8,128)(2,1)} %constant.2.clone.own_band) | copy-start | bytes 196612
  1.0 1.7 %copy-start.3 = (bf16[5,2,8,256]{3,2,1,0:T(8,128)(2,1)S(1)}, bf16[5,2,8,256]{3,2,1,0:T(8,128)(2,1)}, u32[]{:S(2)}) copy-start(bf16[5,2,8,256]{3,2,1,0:T(8,128)(2,1)} %north.1) | copy-start | bytes 122884
  1.0 1.8 %copy-start.4 = (bf16[5,2,8,256]{3,2,1,0:T(8,128)(2,1)S(1)}, bf16[5,2,8,256]{3,2,1,0:T(8,128)(2,1)}, u32[]{:S(2)}) copy-start(bf16[5,2,8,256]{3,2,1,0:T(8,128)(2,1)} %south.1) | copy-start | bytes 122884
  1.0 1.8 %copy-start.5 = (bf16[5,2,256,8]{2,3,1,0:T(8,128)(2,1)S(1)}, bf16[5,2,256,8]{2,3,1,0:T(8,128)(2,1)}, u32[]{:S(2)}) copy-start(bf16[5,2,256,8]{2,3,1,0:T(8,128)(2,1)} %param.17) | copy-start | bytes 122884
  1.0 1.8 %copy-start.6 = (bf16[5,2,256,8]{2,3,1,0:T(8,128)(2,1)S(1)}, bf16[5,2,256,8]{2,3,1,0:T(8,128)(2,1)}, u32[]{:S(2)}) copy-start(bf16[5,2,256,8]{2,3,1,0:T(8,128)(2,1)} %param.18) | copy-start | bytes 122884
  1.0 1.8 %copy-start.9 = (s32[4]{0:T(128)S(1)}, s32[4]{0:T(128)}, u32[]{:S(2)}) copy-start(s32[4]{0:T(128)} %widths.1) | copy-start | bytes 52
  1.0 1.8 %copy-start.10 = (f32[2]{0:T(128)S(1)}, f32[2]{0:T(128)}, u32[]{:S(2)}) copy-start(f32[2]{0:T(128)} %wind_x.1) | copy-start | bytes 28
  1.0 1.8 %copy-start.11 = (f32[2]{0:T(128)S(1)}, f32[2]{0:T(128)}, u32[]{:S(2)}) copy-start(f32[2]{0:T(128)} %wind_y.1) | copy-start | bytes 28
  1.1 1.7 %copy-start.7 = (f32[2,5,5]{2,0,1:T(2,128)S(1)}, f32[2,5,5]{2,0,1:T(2,128)}, u32[]{:S(2)}) copy-start(f32[2,5,5]{2,0,1:T(2,128)} %param.14) | copy-start | bytes 604
  1.1 4.2 %collective-permute-start = (f32[96,128]{1,0:T(8,128)S(1)}, f32[96,128]{1,0:T(8,128)S(1)}, u32[]{:S(2)}, u32[]{:S(2)}) collective-permute-start(f32[96,128]{1,0:T(8,128)S(1)} %get-tuple-element.22), channel_id=1, source_target_pairs={{0,2},{1,3},{2,0},{3,1},{4,6},{5,7},{6,4},{7,5},{8,10},{9,11},{10,... | collective-permute-start | bytes 147464 | tf_op jit(solution)/shard_map/ppermute | solution.py:572
  2.7 0.7 %copy-start.8 = (f32[4,5,2]{1,2,0:T(2,128)S(1)}, f32[4,5,2]{1,2,0:T(2,128)}, u32[]{:S(2)}) copy-start(f32[4,5,2]{1,2,0:T(2,128)} %param.19) | copy-start | bytes 484
  2.7 4.1 %collective-permute-start.1 = (f32[96,128]{1,0:T(8,128)S(1)}, f32[96,128]{1,0:T(8,128)S(1)}, u32[]{:S(2)}, u32[]{:S(2)}) collective-permute-start(f32[96,128]{1,0:T(8,128)S(1)} %get-tuple-element.23), channel_id=1, source_target_pairs={{0,8},{1,9},{2,4},{3,5},{4,2},{5,3},{6,14},{7,15},{8,0},{9,1},{10,... | collective-permute-start | bytes 147464 | tf_op jit(solution)/shard_map/ppermute | solution.py:573
  3.4 5.1 %copy-start.1 = (f32[5,2,64,128]{3,2,1,0:T(8,128)S(1)}, f32[5,2,64,128]{3,2,1,0:T(8,128)}, u32[]{:S(2)}) copy-start(f32[5,2,64,128]{3,2,1,0:T(8,128)} %fields.5) | copy-start | bytes 983044
  7.0 4.0 %collective-permute-start.2 = (f32[64,128]{1,0:T(8,128)S(1)}, f32[64,128]{1,0:T(8,128)S(1)}, u32[]{:S(2)}, u32[]{:S(2)}) collective-permute-start(f32[64,128]{1,0:T(8,128)S(1)} %get-tuple-element.25), channel_id=1, source_target_pairs={{0,1},{1,0},{2,3},{3,2},{4,5},{5,4},{6,7},{7,6},{8,9},{9,8},{10,11... | collective-permute-start | bytes 98312 | tf_op jit(solution)/shard_map/ppermute | solution.py:615

commit v4 on v3

--- a/solution.py
+++ b/solution.py
@@ -265,14 +265,13 @@
 
 def pack_x_kernel(grid_sizes, first_round, second_round, *rest):
     gy_count, gx_count = grid_sizes
-    sides = (len(rest) - 1) // 3
-    payloads, outs, edges, ext = rest[:sides], rest[sides : 2 * sides], rest[2 * sides : -1], rest[-1]
+    sides = (len(rest) - 1) // 2
+    payloads, outs, ext = rest[:sides], rest[sides:-1], rest[-1]
     cols = first_round.shape[1]
     rows = payloads[0].shape[0]
     count = ext.shape[0]
-    lane = iota((2 * PAD, LANES), 1)
+    lane = iota((PAD, LANES), 1)
     starts = sent_starts(gx_count, cols)
-    packed = [jnp.zeros((2 * PAD, LANES), jnp.float32) for _ in starts]
     ext[...] = jnp.zeros_like(ext)
     blocks = [
         [payload[row : row + PAD, :] for row in range(0, rows, PAD)] for payload in payloads
@@ -284,18 +283,13 @@
         ext[index, PAD - HALO : PAD, 0:cols] = north
         ext[index, PAD : PAD + HALO, 0:cols] = south
         for n, start in enumerate(starts):
-            moved = pltpu.roll(ext[index], lax.rem(slot + LANES - start, LANES), 1)
-            packed[n] = jnp.where((lane >= slot) & (lane < slot + HALO), moved, packed[n])
             near = ext[index, FIRST : FIRST + PAD, :]
             moved = pltpu.roll(near, lax.rem(corner + LANES - start, LANES), 1)
-            here = (lane[0:PAD] >= corner) & (lane[0:PAD] < corner + HALO)
+            here = (lane >= corner) & (lane < corner + HALO)
             blocks[n][row // PAD] = jnp.where(here, moved, blocks[n][row // PAD])
-    for n, payload in enumerate(payloads):
+    for n in range(sides):
         for block, value in enumerate(blocks[n]):
             outs[n][block * PAD : (block + 1) * PAD, :] = value
-        edges[n][0:PAD, :] = packed[n][0:PAD]
-        edges[n][PAD : PAD + rows, :] = payload[...]
-        edges[n][PAD + rows : 2 * PAD + rows, :] = packed[n][PAD : 2 * PAD]
 
 
 def loaded(weights, l, fac, count_f):
@@ -358,9 +352,11 @@
     *rest,
 ):
     gy_count, gx_count = grid_sizes
-    sides = (len(rest) - 5) // 4
-    edges, side_drive, after = rest[:sides], rest[sides : 2 * sides], rest[2 * sides]
-    far, edge_one = rest[2 * sides + 1 : 3 * sides + 1], rest[3 * sides + 1 : -4]
+    sides = (len(rest) - 5) // 5
+    payloads, side_drive, after = rest[:sides], rest[sides : 2 * sides], rest[2 * sides]
+    edges, far, edge_one = (
+        rest[2 * sides + 1 + n * sides : 2 * sides + 1 + (n + 1) * sides] for n in range(3)
+    )
     state, own_one, own_two, xdiv = rest[-4:]
     count_f, count_l, rows, cols = fields.shape
     wide_rows = relax.shape[0]
@@ -377,7 +373,17 @@
         state[f, l, PAD : PAD + rows, 0:cols] = fields[f, l]
         state[f, l, PAD + rows : PAD + rows + HALO, 0:cols] = south
     lane = iota((wide_rows, LANES), 1)
-    starts = edge_starts(gx_count, cols)[1]
+    near, starts = edge_starts(gx_count, cols)
+    short = iota((PAD, LANES), 1)
+    for edge, payload, start in zip(edges, payloads, near):
+        edge[PAD : PAD + rows, :] = payload[...]
+        for at in (0, PAD + rows):
+            packed = jnp.zeros((PAD, LANES), jnp.float32)
+            for f, l, slot in slots(count_f, count_l):
+                shift = lax.rem(slot + LANES - start, LANES)
+                moved = pltpu.roll(state[f, l, at : at + PAD, :], shift, 1)
+                packed = jnp.where((short >= slot) & (short < slot + HALO), moved, packed)
+            edge[at : at + PAD, :] = packed
 
     def keep_far(src, section):
         for ref, start in zip(far, starts):
@@ -601,14 +607,13 @@
         prepared[7 + n * sides : 7 + (n + 1) * sides] for n in range(3)
     )
 
-    packed_x = call(
+    sent = call(
         functools.partial(pack_x_kernel, grid_sizes),
         "pack_x",
-        (f32((rows, LANES)),) * sides + (f32((ext_rows, LANES)),) * sides,
+        (f32((rows, LANES)),) * sides,
         inputs(vmem, first_round, second_round, *payloads),
         scratch=[pltpu.VMEM((count_f * count_l, 2 * PAD, LANES), jnp.float32)],
     )
-    sent, edges = packed_x[:sides], packed_x[sides:]
     forward = [(i, i + 1) for i in range(gx_count - 1)]
     backward = [(b, a) for a, b in forward]
     if sides == 1:
@@ -617,13 +622,15 @@
         halos = [lax.ppermute(sent[0], "gx", forward), lax.ppermute(sent[1], "gx", backward)]
 
     state = pltpu.VMEM(state_shape, jnp.float32)
-    edges = edges[::-1]
     after, *begun = call(
         functools.partial(begin_kernel, grid_sizes),
         "begin",
-        (f32(fields.shape),) + (f32((3, wide_rows, LANES)),) * sides + (plane,) * sides,
+        (f32(fields.shape),)
+        + (f32((ext_rows, LANES)),) * sides
+        + (f32((3, wide_rows, LANES)),) * sides
+        + (plane,) * sides,
         inputs(vmem, fields, first_round, second_round, drive, relax, weights, own_matrix)
-        + inputs(vmem, row_relax, lane_weights, *edges, *side_drive),
+        + inputs(vmem, row_relax, lane_weights, *payloads[::-1], *side_drive),
         scratch=[state] * 3 + [pltpu.VMEM((count_f, wide_rows, LANES), jnp.float32)],
         limit=8,
     )
@@ -632,7 +639,7 @@
         functools.partial(finish_kernel, grid_sizes, sides),
         "finish",
         f32(fields.shape),
-        inputs(vmem, *halos, *edges, *begun, *side_drive, *side_matrix)
+        inputs(vmem, *halos, *begun, *side_drive, *side_matrix)
         + inputs(vmem, after, row_relax, inside, lane_weights),
         scratch=[pltpu.VMEM((ext_rows, LANES), jnp.float32), pair, pair],
     )

time: 12.6 us -> 12.6 us (level)
  the two profiles are of different devices: /device:TPU:16 before, /device:TPU:20 now
where the time goes in v4:
time: 12.6 us; the launch traced here: 12.4 us
  Pallas kernels  5.01 us (40%)
  starting transfers between devices  3.2 us (25%)
  waiting for transfers between devices  2.44 us (19%)
  local copies, waits for them, and re-layouts  1.62 us (13%)
  between operations  0.14 us (1%)
    pallas_call x5, Pallas kernels, call(): pl.pallas_call(body, out_shape=out_shape, in_specs=[space for _, space in...  5.01 us
    ppermute x1, starting transfers between devices, local(): first_round = lax.ppermute(sent_first, axes, first_pairs)  1.64 us
    unnamed x24, local copies, waits for them, and re-layouts  1.62 us
    ppermute x1, waiting for transfers between devices, local(): second_round = lax.ppermute(sent_second, axes, second_pairs)  1.58 us
    ppermute x1, starting transfers between devices, local(): halos = [lax.ppermute(sent[0], 'gx', forward + backward)]  1.56 us
    ppermute x1, waiting for transfers between devices, local(): first_round = lax.ppermute(sent_first, axes, first_pairs)  0.6 us
    ppermute x1, waiting for transfers between devices, local(): halos = [lax.ppermute(sent[0], 'gx', forward + backward)]  0.26 us
  transfers between devices with their start and end apart: 3, of which 3 were waited for; matrix products, arithmetic and copies ran while one was open for 0% of the time, Pallas kernels for 27%

profile of v4, /device:TPU:20, one launch (start us, length us, event | category | flops | bytes accessed | tf_op | source)
XLA Modules:
  0.0 12.4 jit_solution(16132610055803839499)
XLA Ops:
  0.0 0.0 copy-start
  0.0 1.0 %copy-done = f32[5,2,64,128]{3,2,1,0:T(8,128)S(1)} copy-done((f32[5,2,64,128]{3,2,1,0:T(8,128)S(1)}, f32[5,2,64,128]{3,2,1,0:T(8,128)}, u32[]{:S(2)}) %copy-start) | copy-done | bytes 327704
  1.0 0.0 copy-start.2
  1.0 0.0 copy-start.3
  1.0 0.0 copy-start.4
  1.0 0.0 copy-start.5
  1.0 0.0 copy-start.6
  1.0 0.0 copy-start.9
  1.0 0.0 copy-start.10
  1.0 0.0 copy-start.11
  1.1 0.0 copy-start.7
  1.1 1.6 %collective-permute-start = (f32[96,128]{1,0:T(8,128)S(1)}, f32[96,128]{1,0:T(8,128)S(1)}, u32[]{:S(2)}, u32[]{:S(2)}) collective-permute-start(f32[96,128]{1,0:T(8,128)S(1)} %get-tuple-element.21), channel_id=1, source_target_pairs={{0,2},{1,3},{2,0},{3,1},{4,6},{5,7},{6,4},{7,5},{8,10},{9,11},{10,... | collective-permute-start | bytes 147464 | tf_op jit(solution)/shard_map/ppermute | solution.py:578
  2.7 0.0 collective-permute-start.1
  2.7 0.0 copy-done.2
  2.7 0.0 copy-done.3
  2.7 0.0 copy-done.4
  2.7 0.0 copy-done.5
  2.7 0.0 copy-done.6
  2.8 0.0 copy-done.9
  2.8 0.0 copy-done.10
  2.8 0.0 copy-done.11
  2.8 0.0 copy-done.7
  2.8 0.6 %copy-done.8 = f32[4,5,2]{1,2,0:T(2,128)S(1)} copy-done((f32[4,5,2]{1,2,0:T(2,128)S(1)}, f32[4,5,2]{1,2,0:T(2,128)}, u32[]{:S(2)}) %copy-start.8) | copy-done | bytes 184
  3.4 1.2 %prepare.1 = (f32[5,2,80,128]{3,2,1,0:T(8,128)S(1)}, f32[80,128]{1,0:T(8,128)S(1)}, f32[80,128]{1,0:T(8,128)S(1)}, f32[80,128]{1,0:T(8,128)S(1)}, f32[2,32,8,128...) custom-call(f32[5,2,64,128]{3,2,1,0:T(8,128)S(1)} %copy-done, ...), custom_call_target="tpu_custom_call" | custom-call | tf_op jit(solution)/shard_map/prepare/pallas_call | solution.py:559
  4.6 0.6 %collective-permute-done.first_round = f32[96,128]{1,0:T(8,128)S(1)} collective-permute-done((f32[96,128]{1,0:T(8,128)S(1)}, f32[96,128]{1,0:T(8,128)S(1)}, u32[]{:S(2)}, u32[]{:S(2)}) %collective-permute-start) | collective-permute-done | bytes 49184 | tf_op jit(solution)/shard_map/ppermute | solution.py:578
  5.2 1.6 %collective-permute-done.1.second_round = f32[96,128]{1,0:T(8,128)S(1)} collective-permute-done((f32[96,128]{1,0:T(8,128)S(1)}, f32[96,128]{1,0:T(8,128)S(1)}, u32[]{:S(2)}, u32[]{:S(2)}) %collective-permute-start.1) | collective-permute-done | bytes 49184 | tf_op jit(solution)/shard_map/ppermute | solution.py:579
  6.8 0.1 pack_x.1
  6.9 1.6 %collective-permute-start.2 = (f32[64,128]{1,0:T(8,128)S(1)}, f32[64,128]{1,0:T(8,128)S(1)}, u32[]{:S(2)}, u32[]{:S(2)}) collective-permute-start(f32[64,128]{1,0:T(8,128)S(1)} %pack_x.1), channel_id=1, source_target_pairs={{0,1},{1,0},{2,3},{3,2},{4,5},{5,4},{6,7},{7,6},{8,9},{9,8},{10,11... | collective-permute-start | bytes 98312 | tf_op jit(solution)/shard_map/ppermute | solution.py:620
  8.5 0.0 copy-done.1
  8.5 2.2 %begin.1 = (f32[5,2,64,128]{3,2,1,0:T(8,128)S(1)}, f32[96,128]{1,0:T(8,128)S(1)}, f32[3,80,128]{2,1,0:T(8,128)S(1)}, f32[80,128]{1,0:T(8,128)S(1)}) custom-call(f32[5,2,64,128]{3,2,1,0:T(8,128)S(1)} %copy-done.1, f32[96,128]{1,0:T(8,128)S(1)} %collective-permute-done.first_round, f32[96,128]{1,0:T(8,128)S(1)} %collective-permute-done.1.second_round, ...), custom_call_target="tpu_custom_call" | custom-call | tf_op jit(solution)/shard_map/begin/pallas_call | solution.py:559
  10.6 0.3 %collective-permute-done.2.refs_0_ = f32[64,128]{1,0:T(8,128)S(1)} collective-permute-done((f32[64,128]{1,0:T(8,128)S(1)}, f32[64,128]{1,0:T(8,128)S(1)}, u32[]{:S(2)}, u32[]{:S(2)}) %collective-permute-start.2) | collective-permute-done | bytes 32800 | tf_op jit(solution)/shard_map/ppermute | solution.py:620
  10.9 1.5 %finish.1 = f32[5,2,64,128]{3,2,1,0:T(8,128)} custom-call(f32[64,128]{1,0:T(8,128)S(1)} %collective-permute-done.2.refs_0_, f32[96,128]{1,0:T(8,128)S(1)} %get-tuple-element.31.refs_1_, f32[3,80,128]{2,1,0:T(8,128)S(1)} %get-tuple-element.32.refs_2_, f32[80,128]{1,0:T(8,128)S(1)} %get-tuple-element.33.refs_3_, ...), custom_call_target="tpu_custom_call" | custom-call | tf_op jit(solution)/shard_map/finish/pallas_call | solution.py:559
  (3 shorter events, 0.0 us)
Async XLA Ops:
  0.0 1.0 %copy-start = (f32[5,2,64,128]{3,2,1,0:T(8,128)S(1)}, f32[5,2,64,128]{3,2,1,0:T(8,128)}, u32[]{:S(2)}) copy-start(f32[5,2,64,128]{3,2,1,0:T(8,128)} %fields.5) | copy-start | bytes 983044
  1.0 1.7 %copy-start.2 = (bf16[2,128,128]{2,1,0:T(8,128)(2,1)S(1)}, bf16[2,128,128]{2,1,0:T(8,128)(2,1)}, u32[]{:S(2)}) copy-start(bf16[2,128,128]{2,1,0:T(8,128)(2,1)} %constant.2.clone.own_band) | copy-start | bytes 196612
  1.0 1.7 %copy-start.3 = (bf16[5,2,8,256]{3,2,1,0:T(8,128)(2,1)S(1)}, bf16[5,2,8,256]{3,2,1,0:T(8,128)(2,1)}, u32[]{:S(2)}) copy-start(bf16[5,2,8,256]{3,2,1,0:T(8,128)(2,1)} %north.1) | copy-start | bytes 122884
  1.0 1.8 %copy-start.4 = (bf16[5,2,8,256]{3,2,1,0:T(8,128)(2,1)S(1)}, bf16[5,2,8,256]{3,2,1,0:T(8,128)(2,1)}, u32[]{:S(2)}) copy-start(bf16[5,2,8,256]{3,2,1,0:T(8,128)(2,1)} %south.1) | copy-start | bytes 122884
  1.0 1.8 %copy-start.5 = (bf16[5,2,256,8]{2,3,1,0:T(8,128)(2,1)S(1)}, bf16[5,2,256,8]{2,3,1,0:T(8,128)(2,1)}, u32[]{:S(2)}) copy-start(bf16[5,2,256,8]{2,3,1,0:T(8,128)(2,1)} %param.17) | copy-start | bytes 122884
  1.0 1.8 %copy-start.6 = (bf16[5,2,256,8]{2,3,1,0:T(8,128)(2,1)S(1)}, bf16[5,2,256,8]{2,3,1,0:T(8,128)(2,1)}, u32[]{:S(2)}) copy-start(bf16[5,2,256,8]{2,3,1,0:T(8,128)(2,1)} %param.18) | copy-start | bytes 122884
  1.0 1.8 %copy-start.9 = (s32[4]{0:T(128)S(1)}, s32[4]{0:T(128)}, u32[]{:S(2)}) copy-start(s32[4]{0:T(128)} %widths.1) | copy-start | bytes 52
  1.0 1.8 %copy-start.10 = (f32[2]{0:T(128)S(1)}, f32[2]{0:T(128)}, u32[]{:S(2)}) copy-start(f32[2]{0:T(128)} %wind_x.1) | copy-start | bytes 28
  1.0 1.8 %copy-start.11 = (f32[2]{0:T(128)S(1)}, f32[2]{0:T(128)}, u32[]{:S(2)}) copy-start(f32[2]{0:T(128)} %wind_y.1) | copy-start | bytes 28
  1.1 1.7 %copy-start.7 = (f32[2,5,5]{2,0,1:T(2,128)S(1)}, f32[2,5,5]{2,0,1:T(2,128)}, u32[]{:S(2)}) copy-start(f32[2,5,5]{2,0,1:T(2,128)} %param.14) | copy-start | bytes 604
  1.1 4.2 %collective-permute-start = (f32[96,128]{1,0:T(8,128)S(1)}, f32[96,128]{1,0:T(8,128)S(1)}, u32[]{:S(2)}, u32[]{:S(2)}) collective-permute-start(f32[96,128]{1,0:T(8,128)S(1)} %get-tuple-element.21), channel_id=1, source_target_pairs={{0,2},{1,3},{2,0},{3,1},{4,6},{5,7},{6,4},{7,5},{8,10},{9,11},{10,... | collective-permute-start | bytes 147464 | tf_op jit(solution)/shard_map/ppermute | solution.py:578
  2.7 0.7 %copy-start.8 = (f32[4,5,2]{1,2,0:T(2,128)S(1)}, f32[4,5,2]{1,2,0:T(2,128)}, u32[]{:S(2)}) copy-start(f32[4,5,2]{1,2,0:T(2,128)} %param.19) | copy-start | bytes 484
  2.7 4.1 %collective-permute-start.1 = (f32[96,128]{1,0:T(8,128)S(1)}, f32[96,128]{1,0:T(8,128)S(1)}, u32[]{:S(2)}, u32[]{:S(2)}) collective-permute-start(f32[96,128]{1,0:T(8,128)S(1)} %get-tuple-element.22), channel_id=1, source_target_pairs={{0,8},{1,9},{2,4},{3,5},{4,2},{5,3},{6,14},{7,15},{8,0},{9,1},{10,... | collective-permute-start | bytes 147464 | tf_op jit(solution)/shard_map/ppermute | solution.py:579
  3.4 5.1 %copy-start.1 = (f32[5,2,64,128]{3,2,1,0:T(8,128)S(1)}, f32[5,2,64,128]{3,2,1,0:T(8,128)}, u32[]{:S(2)}) copy-start(f32[5,2,64,128]{3,2,1,0:T(8,128)} %fields.5) | copy-start | bytes 983044
  6.9 4.0 %collective-permute-start.2 = (f32[64,128]{1,0:T(8,128)S(1)}, f32[64,128]{1,0:T(8,128)S(1)}, u32[]{:S(2)}, u32[]{:S(2)}) collective-permute-start(f32[64,128]{1,0:T(8,128)S(1)} %pack_x.1), channel_id=1, source_target_pairs={{0,1},{1,0},{2,3},{3,2},{4,5},{5,4},{6,7},{7,6},{8,9},{9,8},{10,11... | collective-permute-start | bytes 98312 | tf_op jit(solution)/shard_map/ppermute | solution.py:620

commit v5 on v4

--- a/solution.py
+++ b/solution.py
@@ -437,7 +437,7 @@
     halos, edges, fars, edge_one, side_drive, side_matrix = (
         refs[n * sides : (n + 1) * sides] for n in range(6)
     )
-    after, row_relax, inside, lane_weights, out, outer, one, two = refs[6 * sides :]
+    after, row_relax, inside, lane_weights, out, outer, one, two, ready, sent = refs[6 * sides :]
     count_f, count_l, rows, cols = out.shape
     wide_rows = row_relax.shape[0]
     gx = lax.axis_index("gx")
@@ -514,10 +514,16 @@
         near = (lane >= starts[s]) & (lane < starts[s] + HALO)
         if exists[s] is not None:
             near = near & exists[s]
-        source = after if s == 0 else out
-        for f, l, slot in slots(count_f, count_l):
-            moved = pltpu.roll(right, lax.rem(starts[s] + LANES - slot, LANES), 1)
-            out[f, l] = jnp.where(near[:, 0:cols], moved[:, 0:cols], source[f, l])
+        source = after if s == 0 else ready
+        for f in range(count_f):
+            for l in range(count_l):
+                slot = HALO * (f * count_l + l)
+                moved = pltpu.roll(right, lax.rem(starts[s] + LANES - slot, LANES), 1)
+                ready[f, l] = jnp.where(near[:, 0:cols], moved[:, 0:cols], source[f, l])
+            if s == sides - 1:
+                pltpu.make_async_copy(ready.at[f], out.at[f], sent.at[f]).start()
+    for f in range(count_f):
+        pltpu.make_async_copy(ready.at[f], out.at[f], sent.at[f]).wait()
 
 
 def pair_rounds(part_count, gy_count, gx_count):
@@ -554,13 +560,13 @@
     smem = pl.BlockSpec(memory_space=pltpu.SMEM)
     f32 = functools.partial(jax.ShapeDtypeStruct, dtype=jnp.float32)
 
-    def call(body, name, out_shape, inputs, scratch=(), limit=4):
+    def call(body, name, out_shape, inputs, scratch=(), limit=4, out_space=vmem):
         several = isinstance(out_shape, tuple)
         return pl.pallas_call(
             body,
             out_shape=out_shape,
             in_specs=[space for _, space in inputs],
-            out_specs=(vmem,) * len(out_shape) if several else vmem,
+            out_specs=(out_space,) * len(out_shape) if several else out_space,
             scratch_shapes=list(scratch),
             compiler_params=pltpu.CompilerParams(vmem_limit_bytes=limit << 20),
             name=name,
@@ -641,7 +647,9 @@
         f32(fields.shape),
         inputs(vmem, *halos, *begun, *side_drive, *side_matrix)
         + inputs(vmem, after, row_relax, inside, lane_weights),
-        scratch=[pltpu.VMEM((ext_rows, LANES), jnp.float32), pair, pair],
+        scratch=[pltpu.VMEM((ext_rows, LANES), jnp.float32), pair, pair]
+        + [pltpu.VMEM(fields.shape, jnp.float32), pltpu.SemaphoreType.DMA((count_f,))],
+        out_space=pl.BlockSpec(memory_space=pl.ANY),
     )
 
 

time: 12.6 us -> 12.6 us (level)
  the two profiles are of different devices: /device:TPU:20 before, /device:TPU:16 now
where the time goes in v5:
time: 12.6 us; the launch traced here: 12.4 us
  Pallas kernels  5.03 us (40%)
  starting transfers between devices  3.2 us (25%)
  waiting for transfers between devices  2.45 us (19%)
  local copies, waits for them, and re-layouts  1.62 us (13%)
  between operations  0.14 us (1%)
    pallas_call x5, Pallas kernels, call(): pl.pallas_call(body, out_shape=out_shape, in_specs=[space for _, space in...  5.03 us
    ppermute x1, starting transfers between devices, local(): first_round = lax.ppermute(sent_first, axes, first_pairs)  1.64 us
    unnamed x24, local copies, waits for them, and re-layouts  1.62 us
    ppermute x1, waiting for transfers between devices, local(): second_round = lax.ppermute(sent_second, axes, second_pairs)  1.58 us
    ppermute x1, starting transfers between devices, local(): halos = [lax.ppermute(sent[0], 'gx', forward + backward)]  1.56 us
    ppermute x1, waiting for transfers between devices, local(): first_round = lax.ppermute(sent_first, axes, first_pairs)  0.6 us
    ppermute x1, waiting for transfers between devices, local(): halos = [lax.ppermute(sent[0], 'gx', forward + backward)]  0.27 us
  transfers between devices with their start and end apart: 3, of which 3 were waited for; matrix products, arithmetic and copies ran while one was open for 0% of the time, Pallas kernels for 27%

profile of v5, /device:TPU:16, one launch (start us, length us, event | category | flops | bytes accessed | tf_op | source)
XLA Modules:
  0.0 12.4 jit_solution(9932922347345816076)
XLA Ops:
  0.0 0.0 copy-start
  0.0 1.0 %copy-done = f32[5,2,64,128]{3,2,1,0:T(8,128)S(1)} copy-done((f32[5,2,64,128]{3,2,1,0:T(8,128)S(1)}, f32[5,2,64,128]{3,2,1,0:T(8,128)}, u32[]{:S(2)}) %copy-start) | copy-done | bytes 327704
  1.0 0.0 copy-start.2
  1.0 0.0 copy-start.3
  1.0 0.0 copy-start.4
  1.0 0.0 copy-start.5
  1.0 0.0 copy-start.6
  1.0 0.0 copy-start.9
  1.0 0.0 copy-start.10
  1.0 0.0 copy-start.11
  1.1 0.0 copy-start.7
  1.1 1.6 %collective-permute-start = (f32[96,128]{1,0:T(8,128)S(1)}, f32[96,128]{1,0:T(8,128)S(1)}, u32[]{:S(2)}, u32[]{:S(2)}) collective-permute-start(f32[96,128]{1,0:T(8,128)S(1)} %get-tuple-element.21), channel_id=1, source_target_pairs={{0,2},{1,3},{2,0},{3,1},{4,6},{5,7},{6,4},{7,5},{8,10},{9,11},{10,... | collective-permute-start | bytes 147464 | tf_op jit(solution)/shard_map/ppermute | solution.py:584
  2.7 0.0 collective-permute-start.1
  2.7 0.0 copy-done.2
  2.7 0.0 copy-done.3
  2.7 0.0 copy-done.4
  2.7 0.0 copy-done.5
  2.7 0.0 copy-done.6
  2.8 0.0 copy-done.9
  2.8 0.0 copy-done.10
  2.8 0.0 copy-done.11
  2.8 0.0 copy-done.7
  2.8 0.6 %copy-done.8 = f32[4,5,2]{1,2,0:T(2,128)S(1)} copy-done((f32[4,5,2]{1,2,0:T(2,128)S(1)}, f32[4,5,2]{1,2,0:T(2,128)}, u32[]{:S(2)}) %copy-start.8) | copy-done | bytes 184
  3.4 1.2 %prepare.1 = (f32[5,2,80,128]{3,2,1,0:T(8,128)S(1)}, f32[80,128]{1,0:T(8,128)S(1)}, f32[80,128]{1,0:T(8,128)S(1)}, f32[80,128]{1,0:T(8,128)S(1)}, f32[2,32,8,128...) custom-call(f32[5,2,64,128]{3,2,1,0:T(8,128)S(1)} %copy-done, ...), custom_call_target="tpu_custom_call" | custom-call | tf_op jit(solution)/shard_map/prepare/pallas_call | solution.py:565
  4.6 0.6 %collective-permute-done.first_round = f32[96,128]{1,0:T(8,128)S(1)} collective-permute-done((f32[96,128]{1,0:T(8,128)S(1)}, f32[96,128]{1,0:T(8,128)S(1)}, u32[]{:S(2)}, u32[]{:S(2)}) %collective-permute-start) | collective-permute-done | bytes 49184 | tf_op jit(solution)/shard_map/ppermute | solution.py:584
  5.2 1.6 %collective-permute-done.1.second_round = f32[96,128]{1,0:T(8,128)S(1)} collective-permute-done((f32[96,128]{1,0:T(8,128)S(1)}, f32[96,128]{1,0:T(8,128)S(1)}, u32[]{:S(2)}, u32[]{:S(2)}) %collective-permute-start.1) | collective-permute-done | bytes 49184 | tf_op jit(solution)/shard_map/ppermute | solution.py:585
  6.8 0.1 pack_x.1
  6.9 1.6 %collective-permute-start.2 = (f32[64,128]{1,0:T(8,128)S(1)}, f32[64,128]{1,0:T(8,128)S(1)}, u32[]{:S(2)}, u32[]{:S(2)}) collective-permute-start(f32[64,128]{1,0:T(8,128)S(1)} %pack_x.1), channel_id=1, source_target_pairs={{0,1},{1,0},{2,3},{3,2},{4,5},{5,4},{6,7},{7,6},{8,9},{9,8},{10,11... | collective-permute-start | bytes 98312 | tf_op jit(solution)/shard_map/ppermute | solution.py:626
  8.5 0.0 copy-done.1
  8.5 2.1 %begin.1 = (f32[5,2,64,128]{3,2,1,0:T(8,128)S(1)}, f32[96,128]{1,0:T(8,128)S(1)}, f32[3,80,128]{2,1,0:T(8,128)S(1)}, f32[80,128]{1,0:T(8,128)S(1)}) custom-call(f32[5,2,64,128]{3,2,1,0:T(8,128)S(1)} %copy-done.1, f32[96,128]{1,0:T(8,128)S(1)} %collective-permute-done.first_round, f32[96,128]{1,0:T(8,128)S(1)} %collective-permute-done.1.second_round, ...), custom_call_target="tpu_custom_call" | custom-call | tf_op jit(solution)/shard_map/begin/pallas_call | solution.py:565
  10.6 0.3 %collective-permute-done.2.refs_0_ = f32[64,128]{1,0:T(8,128)S(1)} collective-permute-done((f32[64,128]{1,0:T(8,128)S(1)}, f32[64,128]{1,0:T(8,128)S(1)}, u32[]{:S(2)}, u32[]{:S(2)}) %collective-permute-start.2) | collective-permute-done | bytes 32800 | tf_op jit(solution)/shard_map/ppermute | solution.py:626
  10.9 1.5 %finish.1 = f32[5,2,64,128]{3,2,1,0:T(8,128)} custom-call(f32[64,128]{1,0:T(8,128)S(1)} %collective-permute-done.2.refs_0_, f32[96,128]{1,0:T(8,128)S(1)} %get-tuple-element.31.refs_1_, f32[3,80,128]{2,1,0:T(8,128)S(1)} %get-tuple-element.32.refs_2_, f32[80,128]{1,0:T(8,128)S(1)} %get-tuple-element.33.refs_3_, ...), custom_call_target="tpu_custom_call" | custom-call | tf_op jit(solution)/shard_map/finish/pallas_call | solution.py:565
  (3 shorter events, 0.0 us)
Async XLA Ops:
  0.0 1.0 %copy-start = (f32[5,2,64,128]{3,2,1,0:T(8,128)S(1)}, f32[5,2,64,128]{3,2,1,0:T(8,128)}, u32[]{:S(2)}) copy-start(f32[5,2,64,128]{3,2,1,0:T(8,128)} %fields.5) | copy-start | bytes 983044
  1.0 1.7 %copy-start.2 = (bf16[2,128,128]{2,1,0:T(8,128)(2,1)S(1)}, bf16[2,128,128]{2,1,0:T(8,128)(2,1)}, u32[]{:S(2)}) copy-start(bf16[2,128,128]{2,1,0:T(8,128)(2,1)} %constant.2.clone.own_band) | copy-start | bytes 196612
  1.0 1.7 %copy-start.3 = (bf16[5,2,8,256]{3,2,1,0:T(8,128)(2,1)S(1)}, bf16[5,2,8,256]{3,2,1,0:T(8,128)(2,1)}, u32[]{:S(2)}) copy-start(bf16[5,2,8,256]{3,2,1,0:T(8,128)(2,1)} %north.1) | copy-start | bytes 122884
  1.0 1.8 %copy-start.4 = (bf16[5,2,8,256]{3,2,1,0:T(8,128)(2,1)S(1)}, bf16[5,2,8,256]{3,2,1,0:T(8,128)(2,1)}, u32[]{:S(2)}) copy-start(bf16[5,2,8,256]{3,2,1,0:T(8,128)(2,1)} %south.1) | copy-start | bytes 122884
  1.0 1.8 %copy-start.5 = (bf16[5,2,256,8]{2,3,1,0:T(8,128)(2,1)S(1)}, bf16[5,2,256,8]{2,3,1,0:T(8,128)(2,1)}, u32[]{:S(2)}) copy-start(bf16[5,2,256,8]{2,3,1,0:T(8,128)(2,1)} %param.17) | copy-start | bytes 122884
  1.0 1.8 %copy-start.6 = (bf16[5,2,256,8]{2,3,1,0:T(8,128)(2,1)S(1)}, bf16[5,2,256,8]{2,3,1,0:T(8,128)(2,1)}, u32[]{:S(2)}) copy-start(bf16[5,2,256,8]{2,3,1,0:T(8,128)(2,1)} %param.18) | copy-start | bytes 122884
  1.0 1.8 %copy-start.9 = (s32[4]{0:T(128)S(1)}, s32[4]{0:T(128)}, u32[]{:S(2)}) copy-start(s32[4]{0:T(128)} %widths.1) | copy-start | bytes 52
  1.0 1.8 %copy-start.10 = (f32[2]{0:T(128)S(1)}, f32[2]{0:T(128)}, u32[]{:S(2)}) copy-start(f32[2]{0:T(128)} %wind_x.1) | copy-start | bytes 28
  1.0 1.8 %copy-start.11 = (f32[2]{0:T(128)S(1)}, f32[2]{0:T(128)}, u32[]{:S(2)}) copy-start(f32[2]{0:T(128)} %wind_y.1) | copy-start | bytes 28
  1.1 1.7 %copy-start.7 = (f32[2,5,5]{2,0,1:T(2,128)S(1)}, f32[2,5,5]{2,0,1:T(2,128)}, u32[]{:S(2)}) copy-start(f32[2,5,5]{2,0,1:T(2,128)} %param.14) | copy-start | bytes 604
  1.1 4.2 %collective-permute-start = (f32[96,128]{1,0:T(8,128)S(1)}, f32[96,128]{1,0:T(8,128)S(1)}, u32[]{:S(2)}, u32[]{:S(2)}) collective-permute-start(f32[96,128]{1,0:T(8,128)S(1)} %get-tuple-element.21), channel_id=1, source_target_pairs={{0,2},{1,3},{2,0},{3,1},{4,6},{5,7},{6,4},{7,5},{8,10},{9,11},{10,... | collective-permute-start | bytes 147464 | tf_op jit(solution)/shard_map/ppermute | solution.py:584
  2.7 0.7 %copy-start.8 = (f32[4,5,2]{1,2,0:T(2,128)S(1)}, f32[4,5,2]{1,2,0:T(2,128)}, u32[]{:S(2)}) copy-start(f32[4,5,2]{1,2,0:T(2,128)} %param.19) | copy-start | bytes 484
  2.7 4.1 %collective-permute-start.1 = (f32[96,128]{1,0:T(8,128)S(1)}, f32[96,128]{1,0:T(8,128)S(1)}, u32[]{:S(2)}, u32[]{:S(2)}) collective-permute-start(f32[96,128]{1,0:T(8,128)S(1)} %get-tuple-element.22), channel_id=1, source_target_pairs={{0,8},{1,9},{2,4},{3,5},{4,2},{5,3},{6,14},{7,15},{8,0},{9,1},{10,... | collective-permute-start | bytes 147464 | tf_op jit(solution)/shard_map/ppermute | solution.py:585
  3.4 5.1 %copy-start.1 = (f32[5,2,64,128]{3,2,1,0:T(8,128)S(1)}, f32[5,2,64,128]{3,2,1,0:T(8,128)}, u32[]{:S(2)}) copy-start(f32[5,2,64,128]{3,2,1,0:T(8,128)} %fields.5) | copy-start | bytes 983044
  6.9 4.0 %collective-permute-start.2 = (f32[64,128]{1,0:T(8,128)S(1)}, f32[64,128]{1,0:T(8,128)S(1)}, u32[]{:S(2)}, u32[]{:S(2)}) collective-permute-start(f32[64,128]{1,0:T(8,128)S(1)} %pack_x.1), channel_id=1, source_target_pairs={{0,1},{1,0},{2,3},{3,2},{4,5},{5,4},{6,7},{7,6},{8,9},{9,8},{10,11... | collective-permute-start | bytes 98312 | tf_op jit(solution)/shard_map/ppermute | solution.py:626
